TPU v7x, 256 devices: a whole 4x4x8 slice. The times are simulated.
256 devices in a mesh: particle: 4 (over y_hi, core), tile: 64 (over y_lo, z, x).
Axes of the slice: x: 4, y: 4 (y_hi: 2, y_lo: 2; y = y_hi * 2 + y_lo), z: 8, core: 2. Of those that a mesh axis runs over, the one named last changes fastest.
Arguments:
- ensemble: float32 [8, 8, 1024, 2048], P('particle', None, 'tile'), may hold values from -6 to 6
- owners: int32 [8], replicated, may hold values from 0 to 7, as said below
- velocity_x: float32 [8, 1024, 2048], P(None, 'tile'), may hold values from -0.3 to 0.3
- northward_speed_ratio: float32 [8, 1024, 2048], P(None, 'tile'), may hold values from -0.3 to 0.3
- target: float32 [8, 1024, 2048], P(None, 'tile'), may hold values from -6 to 6
- forcing: bfloat16 [2, 8, 8, 1024, 2048], P(None, 'particle', None, 'tile'), may hold values from -6 to 6
- diffusion: float32 [8], replicated, may hold values from 0.05 to 0.2
- nudging: float32 [8], replicated, may hold values from 0.05 to 0.5
- level_depths: float32 [8], replicated, may hold values from 0.25 to 1
Outputs:
- predicted_ensemble_grids: float32 [8, 8, 2048, 1024], P('particle', None, 'tile')
- northward_flux_scaled: float32 [8, 2048, 1024], P('particle', 'tile')
Inputs may be any that keep to these rules, and one draw needn't show every extreme that they name: `owners`: 0 and 7 always occur; other members are copied any number of times.
All inputs are finite; a program needn't handle non-finite values.
Results may differ from a plain program's by a relative error of at most 0.0003.
Values sent between devices are 32-bit elements; how exact they have to be, the bound alone decides.
No kernel may reach another device: no remote copies, remote signals or barrier semaphores. Data moves between devices by JAX's collectives and lax.ppermute only.
A program may use at most 128 MiB of HBM per device.

v0:
```python
import jax
import jax.numpy as jnp
from jax import lax
from jax.sharding import PartitionSpec as P

forcing_scale = 0.5


def with_halo(value, sides, width):
    for axis, dim in sides:
        size, length = (lax.axis_size(axis), value.shape[dim])
        up = [(i, (i + 1) % size) for i in range(size - 1)]
        down = [(j, i) for i, j in up]
        last = lax.slice_in_dim(value, length - width, length, axis=dim)
        leading = lax.slice_in_dim(value, 0, width, axis=dim)
        before = lax.ppermute(last, axis, up)
        after = lax.ppermute(leading, axis, down)
        value = jnp.concatenate([before, value, after], axis=dim)
    return value


def advance(padded, velocity_x, northward_speed_ratio, diffusion, nudging, target, forcing_now):
    center = padded[..., 1:-1, :]
    northern = padded[..., 2:, :]
    southern = padded[..., :-2, :]
    eastern = jnp.roll(center, -1, axis=-1)
    west_boundary = jnp.roll(center, 1, axis=-1)
    laplace = eastern + west_boundary + northern + southern - 4.0 * center
    advect = 0.5 * velocity_x * (eastern - west_boundary) + 0.5 * northward_speed_ratio * (
        northern - southern
    )
    return (
        center
        - advect
        + diffusion[:, None, None] * laplace
        + nudging[:, None, None] * (target - center)
        + forcing_scale * forcing_now.astype(jnp.float32)
    )


def select(wanted_ids, arrived):
    arrived_count = arrived.shape[0]
    candidates = jnp.arange(arrived_count, dtype=jnp.int32)
    matches = (wanted_ids[:, None] == candidates[None, :]).astype(jnp.float32)
    return jnp.einsum("jk,klrx->jlrx", matches, arrived, precision=lax.Precision.HIGHEST)


def on_device(
    ensemble,
    owners,
    velocity_x,
    northward_speed_ratio,
    target,
    forcing,
    diffusion,
    nudging,
    level_depths,
):
    per_group = ensemble.shape[0]
    member_group = lax.axis_index("particle")
    wanted = lax.dynamic_slice_in_dim(owners, member_group * per_group, per_group)
    prognostic_tracer = select(wanted, lax.all_gather(ensemble, "particle", axis=0, tiled=True))
    steps_total = forcing.shape[0]
    for step_index in range(steps_total):
        padded = with_halo(prognostic_tracer, (("tile", 2),), 1)
        prognostic_tracer = advance(
            padded,
            velocity_x,
            northward_speed_ratio,
            diffusion,
            nudging,
            target,
            forcing[step_index],
        )
    turned = jnp.transpose(prognostic_tracer, (0, 1, 3, 2))
    arrived = lax.all_to_all(turned, "tile", split_axis=2, concat_axis=3, tiled=True)
    vertical_profile = jnp.sum(level_depths[None, :, None, None] * arrived, axis=1)
    northward_flux_scaled = jnp.cumsum(vertical_profile, axis=2) * arrived.shape[3] ** (-0.5)
    return (arrived, northward_flux_scaled)


def solution(mesh):
    placed = (
        P("particle", None, "tile", None),
        P(),
        P(None, "tile", None),
        P(None, "tile", None),
        P(None, "tile", None),
        P(None, "particle", None, "tile", None),
        P(),
        P(),
        P(),
    )
    return jax.shard_map(
        on_device,
        mesh=mesh,
        in_specs=placed,
        out_specs=(P("particle", None, "tile", None), P("particle", "tile", None)),
        check_vma=False,
    )
```

profile of v0, /device:TPU:6, one launch (start us, length us, event | category | flops | bytes accessed | tf_op | source)
XLA Modules:
  0.0 299.4 jit_solution(12414906669033529263)
XLA Ops:
  7.2 0.7 all-gather.2.cloned.1.call-update
  8.0 0.4 copy-done.4
  8.4 1.5 broadcast_multiply_fusion
  10.0 0.3 copy-done.3
  10.3 2.6 convert_multiply_fusion.1
  12.9 64.7 %all-gather.2.cloned.1.call-done = f32[8,8,16,2048]{3,2,1,0:T(8,128)} async-done(((f32[2,8,16,2048]{3,2,1,0:T(8,128)}), f32[8,8,16,2048]{3,2,1,0:T(8,128)}) %all-gather.2.cloned.1.call-update) | async-done | bytes 8388624 | tf_op jit(solution)/shard_map/all_gather | solution.py:62
  77.6 11.9 %fusion.1 = f32[2,8,16,2048]{3,0,2,1:T(2,128)S(1)} fusion(f32[8,8,16,2048]{3,2,1,0:T(8,128)} %all-gather.2.cloned.1.call-done, s32[2]{0:T(128)S(1)} %dynamic_slice.3), kind=kOutput, calls=%fused_computation.2 | convolution fusion | flops 50331664 | bytes 10485768 | tf_op jit(solution)/shard_map/jk,klrx->jlrx/dot_general | solution.py:45
  89.6 2.4 fusion.13
  92.0 3.6 %collective-permute-start.1 = (f32[2,8,1,2048]{3,0,2,1:T(2,128)S(1)}, f32[2,8,1,2048]{3,0,2,1:T(2,128)S(1)}, u32[]{:S(2)}, u32[]{:S(2)}) collective-permute-start(f32[2,8,1,2048]{3,0,2,1:T(2,128)S(1)} %get-tuple-element.18), channel_id=1, source_target_pairs={{0,1},{1,2},{2,3},{3,4},{4,5},{5,6},{6,7},{7,8},{8,9},{9,10},{10,1... | collective-permute-start | bytes 393224 | tf_op jit(solution)/shard_map/ppermute | solution.py:16
  95.6 2.4 collective-permute-start
  98.2 1.5 collective-permute-done.1
  99.7 5.3 %collective-permute-done = f32[2,8,1,2048]{3,0,2,1:T(2,128)S(1)} collective-permute-done((f32[2,8,1,2048]{3,0,2,1:T(2,128)S(1)}, f32[2,8,1,2048]{3,0,2,1:T(2,128)S(1)}, u32[]{:S(2)}, u32[]{:S(2)}) %collective-permute-start) | collective-permute-done | bytes 131104 | tf_op jit(solution)/shard_map/ppermute | solution.py:17
  105.0 8.0 %fusion.5 = f32[2,8,16,2048]{3,0,2,1:T(2,128)S(1)} fusion(f32[1,2,8,16,2048]{4,3,2,1,0:T(8,128)S(1)} %copy-done.1, f32[2,8,16,2048]{3,0,2,1:T(2,128)S(1)} %fusion.1, f32[2,8,1,2048]{3,0,2,1:T(2,128)S(1)} %collective-permute-done, f32[2,8,1,2048]{3,0,2,1:T(2,128)S(1)} %collective-permute-done.1, f32[2,8,16,2047]{3,0,2,1:T(2,128)S(1)} %get-tuple-element.15, ...), kind=kLoop, calls=%fused_computation.9 | loop fusion | flops 11010048 | bytes 13893696 | tf_op jit(solution)/shard_map/add | solution.py:33
  113.0 2.4 fusion.10
  115.4 1.9 collective-permute-start.3
  117.4 3.9 %collective-permute-start.2 = (f32[2,8,1,2048]{3,0,2,1:T(2,128)S(1)}, f32[2,8,1,2048]{3,0,2,1:T(2,128)S(1)}, u32[]{:S(2)}, u32[]{:S(2)}) collective-permute-start(f32[2,8,1,2048]{3,0,2,1:T(2,128)S(1)} %get-tuple-element.13), channel_id=1, source_target_pairs={{1,0},{2,1},{3,2},{4,3},{5,4},{6,5},{7,6},{8,7},{9,8},{10,9},{11,1... | collective-permute-start | bytes 393224 | tf_op jit(solution)/shard_map/ppermute | solution.py:17
  121.5 0.8 collective-permute-done.3
  122.3 4.0 %collective-permute-done.2 = f32[2,8,1,2048]{3,0,2,1:T(2,128)S(1)} collective-permute-done((f32[2,8,1,2048]{3,0,2,1:T(2,128)S(1)}, f32[2,8,1,2048]{3,0,2,1:T(2,128)S(1)}, u32[]{:S(2)}, u32[]{:S(2)}) %collective-permute-start.2) | collective-permute-done | bytes 131104 | tf_op jit(solution)/shard_map/ppermute | solution.py:17
  126.3 8.7 %fusion.4 = f32[2,8,2048,16]{2,0,3,1:T(2,128)} fusion(f32[1,2,8,16,2048]{4,3,2,1,0:T(8,128)S(1)} %copy-done, f32[2,8,16,2048]{3,0,2,1:T(2,128)S(1)} %fusion.5, f32[2,8,1,2048]{3,0,2,1:T(2,128)S(1)} %collective-permute-done.2, f32[2,8,1,2048]{3,0,2,1:T(2,128)S(1)} %collective-permute-done.3, f32[2,8,16,2047]{3,0,2,1:T(2,128)S(1)} %get-tuple-element.9, ...), kind=kLoop, calls=%fused_computation.6 | loop fusion | flops 11010048 | bytes 13893696 | tf_op jit(solution)/shard_map/transpose | solution.py:75
  135.1 11.9 %copy.38 = f32[2,8,2048,16]{3,1,0,2:T(8,128)} copy(f32[2,8,2048,16]{2,0,3,1:T(2,128)} %fusion.4) | data formatting | bytes 4194304 | tf_op jit(solution)/shard_map/transpose | solution.py:75
  147.0 11.4 %reshape.34 = f32[64,1,8192]{2,1,0:T(1,128)S(1)} reshape(f32[2048,2,8,16]{3,2,1,0:T(8,128)} %bitcast.33) | data formatting | bytes 4194304
  158.3 60.1 %all_to_all.18 = f32[64,1,8192]{2,1,0:T(1,128)} all-to-all(f32[64,1,8192]{2,1,0:T(1,128)S(1)} %reshape.34), channel_id=1, replica_groups=mesh['particle'=4,'tile'=64] {'tile'}, dimensions={0} | all-to-all | bytes 4194304 | tf_op jit(solution)/shard_map/all_to_all | solution.py:76
  218.4 0.5 broadcast.39
  218.9 7.5 %reduce.1 = f32[64,8192]{1,0:T(8,128)S(1)} reduce(f32[64,1,8192]{2,1,0:T(1,128)} %all_to_all.18, f32[]{:T(128)} %broadcast.39), dimensions={1}, to_apply=%all_to_all.13.reduce_sub_computation | reduce | bytes 4194308 | tf_op jit(solution)/shard_map/all_to_all | solution.py:76
  226.5 8.9 %reshape.35 = f32[2048,2,8,16]{3,2,1,0:T(8,128)} reshape(f32[64,8192]{1,0:T(8,128)S(1)} %reduce.1) | data formatting | bytes 4194304
  235.4 13.1 %copy.47 = f32[2,8,64,32,16]{3,2,4,1,0:T(8,128)} copy(f32[2,8,64,32,16]{4,1,0,3,2:T(8,128)} %bitcast.31) | data formatting | bytes 4194304 | tf_op jit(solution)/shard_map/all_to_all | solution.py:76
  248.5 4.6 %fusion = f32[2,32,64,16]{1,2,3,0:T(8,128)S(1)} fusion(f32[2,8,64,32,16]{3,2,4,1,0:T(8,128)} %copy.47, f32[8]{0:T(128)S(1)} %copy-done.7), kind=kLoop, calls=%fused_computation.1 | loop fusion | flops 983040 | bytes 2359328 | tf_op jit(solution)/shard_map/reduce_sum | solution.py:77
  253.1 0.6 copy.41
  254.1 18.0 %reduce-window.6 = f32[2,32,8,128]{3,2,1,0:T(8,128)S(1)} reduce-window(f32[2,32,8,128]{3,2,1,0:T(8,128)S(1)} %copy.42, f32[]{:T(128)} %constant.22.clone.1), window={size=1x1x1x128 pad=0_0x0_0x0_0x127_0}, to_apply=%region_1.2 | reduce-window | flops 8323072 | bytes 524292 | tf_op jit(solution)/shard_map/reduce-window
  272.7 0.7 mul.128
  273.4 12.8 %copy.40 = f32[2,8,32,64,16]{2,4,3,1,0:T(8,128)} copy(f32[2,8,32,64,16]{4,1,0,2,3:T(8,128)} %bitcast.32) | data formatting | bytes 4194304 | tf_op jit(solution)/shard_map/all_to_all | solution.py:76
  286.3 6.2 %copy.45 = f32[2,8,32,1024]{3,2,1,0:T(8,128)} copy(f32[2,8,32,1024]{2,3,1,0:T(8,128)} %bitcast.34) | data formatting | bytes 4194304
  (29 shorter events, 1.5 us)
Async XLA Ops:
  7.2 0.8 copy-start.8
  7.2 1.2 copy-start.4
  7.2 70.4 %all-gather.2.cloned.1.call-start = ((), (), s32[]{:S(2)}) async-start(), calls=%async_computation.1 | async-start | bytes 10485760 | tf_op jit(solution)/shard_map/all_gather | solution.py:62
  8.4 1.9 copy-start.3
  89.5 15.5 %copy-start.1 = (f32[1,2,8,16,2048]{4,3,2,1,0:T(8,128)S(1)}, f32[1,2,8,16,2048]{4,3,2,1,0:T(8,128)}, u32[]{:S(2)}) copy-start(f32[1,2,8,16,2048]{4,3,2,1,0:T(8,128)} %get-tuple-element.20) | copy-start | bytes 6291460
  89.5 15.5 %copy-start.2 = (f32[8,16,2048]{2,1,0:T(8,128)S(1)}, f32[8,16,2048]{2,1,0:T(8,128)}, u32[]{:S(2)}) copy-start(f32[8,16,2048]{2,1,0:T(8,128)} %param.13) | copy-start | bytes 3145732
  89.6 15.4 %copy-start.5 = (f32[8]{0:T(128)S(1)}, f32[8]{0:T(128)}, u32[]{:S(2)}) copy-start(f32[8]{0:T(128)} %param.16) | copy-start | bytes 100
  89.6 15.4 %copy-start.6 = (f32[8]{0:T(128)S(1)}, f32[8]{0:T(128)}, u32[]{:S(2)}) copy-start(f32[8]{0:T(128)} %param.15) | copy-start | bytes 100
  92.0 7.7 %collective-permute-start.1 = (f32[2,8,1,2048]{3,0,2,1:T(2,128)S(1)}, f32[2,8,1,2048]{3,0,2,1:T(2,128)S(1)}, u32[]{:S(2)}, u32[]{:S(2)}) collective-permute-start(f32[2,8,1,2048]{3,0,2,1:T(2,128)S(1)} %get-tuple-element.18), channel_id=1, source_target_pairs={{0,1},{1,2},{2,3},{3,4},{4,5},{5,6},{6,7},{7,8},{8,9},{9,10},{10,1... | collective-permute-start | bytes 393224 | tf_op jit(solution)/shard_map/ppermute | solution.py:16
  95.6 9.4 %collective-permute-start = (f32[2,8,1,2048]{3,0,2,1:T(2,128)S(1)}, f32[2,8,1,2048]{3,0,2,1:T(2,128)S(1)}, u32[]{:S(2)}, u32[]{:S(2)}) collective-permute-start(f32[2,8,1,2048]{3,0,2,1:T(2,128)S(1)} %get-tuple-element.19), channel_id=1, source_target_pairs={{1,0},{2,1},{3,2},{4,3},{5,4},{6,5},{7,6},{8,7},{9,8},{10,9},{11,1... | collective-permute-start | bytes 393224 | tf_op jit(solution)/shard_map/ppermute | solution.py:17
  113.0 13.3 %copy-start = (f32[1,2,8,16,2048]{4,3,2,1,0:T(8,128)S(1)}, f32[1,2,8,16,2048]{4,3,2,1,0:T(8,128)}, u32[]{:S(2)}) copy-start(f32[1,2,8,16,2048]{4,3,2,1,0:T(8,128)} %get-tuple-element.21) | copy-start | bytes 6291460
  115.4 6.9 %collective-permute-start.3 = (f32[2,8,1,2048]{3,0,2,1:T(2,128)S(1)}, f32[2,8,1,2048]{3,0,2,1:T(2,128)S(1)}, u32[]{:S(2)}, u32[]{:S(2)}) collective-permute-start(f32[2,8,1,2048]{3,0,2,1:T(2,128)S(1)} %get-tuple-element.12), channel_id=1, source_target_pairs={{0,1},{1,2},{2,3},{3,4},{4,5},{5,6},{6,7},{7,8},{8,9},{9,10},{10,1... | collective-permute-start | bytes 393224 | tf_op jit(solution)/shard_map/ppermute | solution.py:16
  117.4 9.0 %collective-permute-start.2 = (f32[2,8,1,2048]{3,0,2,1:T(2,128)S(1)}, f32[2,8,1,2048]{3,0,2,1:T(2,128)S(1)}, u32[]{:S(2)}, u32[]{:S(2)}) collective-permute-start(f32[2,8,1,2048]{3,0,2,1:T(2,128)S(1)} %get-tuple-element.13), channel_id=1, source_target_pairs={{1,0},{2,1},{3,2},{4,3},{5,4},{6,5},{7,6},{8,7},{9,8},{10,9},{11,1... | collective-permute-start | bytes 393224 | tf_op jit(solution)/shard_map/ppermute | solution.py:17
  235.4 13.1 %copy-start.7 = (f32[8]{0:T(128)S(1)}, f32[8]{0:T(128)}, u32[]{:S(2)}) copy-start(f32[8]{0:T(128)} %param.17) | copy-start | bytes 100
Sparse Core Ops, SparseCore 0:
  9.8 67.7 all-gather.1
where the time goes:
time: 300 us; the launch traced here: 299 us
  waiting for transfers between devices  77 us (26%)
  local copies, waits for them, and re-layouts  73 us (24%)
  blocking collectives  60.1 us (20%)
  other arithmetic  51.2 us (17%)
  between operations  14.3 us (5%)
  starting transfers between devices  11.9 us (4%)
  matrix products  11.9 us (4%)
    all_gather x1, waiting for transfers between devices, on_device(): lax.all_gather(ensemble, 'particle', axis=0, tiled=True)  64.7 us
    all_to_all x1, blocking collectives, on_device(): lax.all_to_all(turned, 'tile', split_axis=2, concat_axis=3, tiled=True)  60.1 us
    unnamed x21, local copies, waits for them, and re-layouts  27.3 us
    all_to_all x3, local copies, waits for them, and re-layouts, on_device(): lax.all_to_all(turned, 'tile', split_axis=2, concat_axis=3, tiled=True)  26.5 us
    another operation x2, other arithmetic  18.1 us
    transpose x1, local copies, waits for them, and re-layouts, on_device(): turned = jnp.transpose(prognostic_tracer, (0, 1, 3, 2))  11.9 us
    dot_general x1, matrix products, select(): jnp.einsum('jk,klrx->jlrx', matches, arrived, precision=lax.Precision.HIG...  11.9 us
    ppermute x2, waiting for transfers between devices, with_halo(): after = lax.ppermute(leading, axis, down)  9.32 us
  transfers between devices with their start and end apart: 5, of which 5 were waited for; matrix products, arithmetic and copies ran while one was open for 2% of the time, Pallas kernels for 0%

commit v1 on v0

v1 whole, which is shorter than its diff:
```python
import jax
import jax.numpy as jnp
from jax import lax
from jax.experimental import pallas as pl
from jax.experimental.pallas import tpu as pltpu
from jax.sharding import PartitionSpec as P


forcing_scale = 0.5
F32 = jnp.float32
MIB = 1 << 20


def params(limit):
    return pltpu.CompilerParams(vmem_limit_bytes=limit * MIB)


def cost(flops, nbytes):
    return pl.CostEstimate(flops=flops, bytes_accessed=nbytes, transcendentals=0)


def combine(f, east, west, n, so, coefs):
    cc, ce, cw, cn, cs = coefs
    return cc * f + (ce * east + cw * west) + (cn * n + cs * so)


def coefs_of(d, nu, u, v):
    hu = 0.5 * u
    hv = 0.5 * v
    return 1.0 - 4.0 * d - nu, d - hu, d + hu, d - hv, d + hv


def sweep(load, edges, coefs, emit, count, lanes, rows):
    row_id = lax.broadcasted_iota(jnp.int32, (rows, 128), 0)
    lane = lax.broadcasted_iota(jnp.int32, (rows, 128), 1)
    turned = []
    for m in range(count):
        last, first = load(m, lanes - 1), load(m, 0)
        turned.append((first, pltpu.roll(last, 1, 1), pltpu.roll(first, 127, 1), pltpu.roll(first, 1, 1)))
    for j in range(lanes):
        now = coefs(j)
        for m in range(count):
            f, prev_right, here_left, here_right = turned[m]
            following = load(m, (j + 1) % lanes)
            next_left = pltpu.roll(following, 127, 1)
            next_right = pltpu.roll(following, 1, 1)
            east = jnp.where(lane == 127, next_left, here_left)
            west = jnp.where(lane == 0, prev_right, here_right)
            turned[m] = (following, here_right, next_left, next_right)
            low, high = edges(m, j)
            up = jnp.where(row_id == rows - 1, high, pltpu.roll(f, rows - 1, 0))
            down = jnp.where(row_id == 0, low, pltpu.roll(f, 1, 0))
            emit(m, j, combine(f, east, west, up, down, now))


def at(j):
    return slice(128 * j, 128 * j + 128)


def table(shape):
    return pl.BlockSpec(shape, lambda *args: (0,) * len(shape))


def pack_static(scal, vx, vy, target, forcing):
    levels, rows, nx = target.shape

    def body(s, u_ref, v_ref, t_ref, w_ref, up_ref, down_ref):
        for ref, r in ((up_ref, rows - 1), (down_ref, 0)):
            for l in range(levels):
                ref[l : l + 1] = u_ref[l, r : r + 1]
                ref[levels + l : levels + l + 1] = v_ref[l, r : r + 1]
                nt = s[8 + l] * t_ref[l, r : r + 1]
                for m in range(2):
                    w = w_ref[0, m, l].astype(F32)[r : r + 1]
                    i = (2 + m) * levels + l
                    ref[i : i + 1] = nt + forcing_scale * w

    shape = (4 * levels, nx)
    out = jax.ShapeDtypeStruct(shape, F32)
    return pl.pallas_call(
        body,
        name="pack_static",
        out_shape=(out, out),
        grid_spec=pltpu.PrefetchScalarGridSpec(
            num_scalar_prefetch=1,
            grid=(1,),
            in_specs=[table(vx.shape)] * 3 + [table((1,) + forcing.shape[1:])],
            out_specs=[table(shape)] * 2,
        ),
        compiler_params=params(60),
        cost_estimate=cost(0, 16 * target.size),
    )(scal, vx, vy, target, forcing)


def pack_edges(ids, parts, limit):
    rows, nx = parts[0].shape[2:]
    total = 8 * len(parts)

    def body(s, *refs):
        up_ref, down_ref = refs[-2:]
        for p, f_ref in enumerate(refs[:-2]):
            for m in range(2):
                for l in range(2):
                    i = ((2 * p + m) * 2 + l) * 2
                    up_ref[i : i + 2] = f_ref[m, l, rows - 2 : rows]
                    down_ref[i : i + 2] = f_ref[m, l, 0:2]

    block = (2, 2, rows, nx)
    in_specs = []
    for part in parts:
        if part.shape[1] == 2:
            in_specs.append(table(block))
        else:
            in_specs.append(pl.BlockSpec(block, lambda i, s: (0, s[8], 0, 0)))
    out = jax.ShapeDtypeStruct((total, nx), F32)
    return pl.pallas_call(
        body,
        name="pack_edges",
        out_shape=(out, out),
        grid_spec=pltpu.PrefetchScalarGridSpec(
            num_scalar_prefetch=1,
            grid=(1,),
            in_specs=in_specs,
            out_specs=[table((total, nx))] * 2,
        ),
        compiler_params=params(limit),
        cost_estimate=cost(0, len(parts) * 16 * rows * nx),
    )(ids, *parts)


def twice(ids, scal, parts, vx, vy, halo, static, before):
    level_count, rows, nx = vx.shape
    lanes = nx // 128
    base = 0 if before is None else 2

    def body(q, s, f0_ref, f1_ref, u_ref, v_ref, below_ref, above_ref, sb_ref, sa_ref, *rest):
        out_ref, cur_ref, mid_ref, low_ref, high_ref = rest[-5:]
        l, p = pl.program_id(0), pl.program_id(1)
        level = 2 * q[8] + l
        d, nu = s[level], s[8 + level]
        low_ok = s[16] > 0.0
        high_ok = s[17] > 0.0

        @pl.when(p == 0)
        def _():
            cur_ref[...] = f0_ref[:, 0]

        @pl.when(p == 1)
        def _():
            cur_ref[...] = f1_ref[:, 0]

        def edge_row(ref, f, n, so):
            u = ref[pl.ds(level, 1), :]
            v = ref[pl.ds(level_count + level, 1), :]
            east = pltpu.roll(f, nx - 1, 1)
            west = pltpu.roll(f, 1, 1)
            return combine(f, east, west, n, so, coefs_of(d, nu, u, v))

        for m in range(2):
            here = ((2 * p + m) * 2 + l) * 2
            s2 = below_ref[pl.ds(here, 1), :]
            s1 = below_ref[pl.ds(here + 1, 1), :]
            n1 = above_ref[pl.ds(here, 1), :]
            n2 = above_ref[pl.ds(here + 1, 1), :]
            new_low = edge_row(sb_ref, s1, cur_ref[m, 0:1, :], s2)
            new_high = edge_row(sa_ref, n1, n2, cur_ref[m, rows - 1 : rows, :])
            low_ref[0, m] = s1
            high_ref[0, m] = n1
            low_ref[1, m] = jnp.where(low_ok, new_low, 0.0)
            high_ref[1, m] = jnp.where(high_ok, new_high, 0.0)

        def coefs(j):
            return coefs_of(d, nu, u_ref[0, :, at(j)], v_ref[0, :, at(j)])

        for step in range(2):

            def load(m, j):
                return mid_ref[m, :, at(j)] if step else cur_ref[m, :, at(j)]

            def edges(m, j):
                return low_ref[step, m, :, at(j)], high_ref[step, m, :, at(j)]

            def emit(m, j, value):
                if step:
                    out_ref[m, 0, :, at(j)] = value
                else:
                    mid_ref[m, :, at(j)] = value

            sweep(load, edges, coefs, emit, 2, lanes, rows)

    one = pl.BlockSpec((1, rows, nx), lambda l, p, q, s: (2 * q[8] + l, 0, 0))
    part_specs = []
    for part in parts:
        if part.shape[1] == 2:
            part_specs.append(pl.BlockSpec((2, 1, rows, nx), lambda l, p, q, s: (0, l, 0, 0)))
        else:
            part_specs.append(
                pl.BlockSpec((2, 1, rows, nx), lambda l, p, q, s: (0, 2 * q[8] + l, 0, 0))
            )
    in_specs = part_specs + [one, one] + [table(h.shape) for h in (*halo, *static)]
    args = [ids, scal, *parts, vx, vy, *halo, *static]
    aliases = {}
    if before is not None:
        aliases = {len(args): 0}
        in_specs.append(pl.BlockSpec(memory_space=pl.ANY))
        args.append(before)
    return pl.pallas_call(
        body,
        name="twice",
        out_shape=jax.ShapeDtypeStruct((8, 2, rows, nx), F32),
        grid_spec=pltpu.PrefetchScalarGridSpec(
            num_scalar_prefetch=2,
            grid=(2, 2),
            in_specs=in_specs,
            out_specs=pl.BlockSpec((2, 1, rows, nx), lambda l, p, q, s: (base + p, l, 0, 0)),
            scratch_shapes=[
                pltpu.VMEM((2, rows, nx), F32),
                pltpu.VMEM((2, rows, nx), F32),
                pltpu.VMEM((2, 2, 1, nx), F32),
                pltpu.VMEM((2, 2, 1, nx), F32),
            ],
        ),
        input_output_aliases=aliases,
        compiler_params=params(16),
        cost_estimate=cost(60 * 8 * rows * nx, 96 * rows * nx),
    )(*args)


def driven(ids, scal, vx, vy, target, forcing, below, above):
    level_count, rows, nx = target.shape
    lanes = nx // 128

    def body(q, s, u_ref, v_ref, t_ref, w_ref, below_ref, above_ref, *rest):
        outs, (src_ref, res_ref, low_ref, high_ref) = rest[:4], rest[4:]
        k, l = 3 - pl.program_id(0), pl.program_id(1)
        level = 2 * q[8 + k] + l
        d, nu = s[level], s[8 + level]
        for m in range(2):
            low_ref[m] = below_ref[pl.ds((2 + m) * level_count + level, 1), :]
            high_ref[m] = above_ref[pl.ds((2 + m) * level_count + level, 1), :]
        for j in range(lanes):
            nt = nu * t_ref[0, :, at(j)]
            for m in range(2):
                src_ref[m, :, at(j)] = nt + forcing_scale * w_ref[0, m, 0, :, at(j)].astype(F32)

        def coefs(j):
            return coefs_of(d, nu, u_ref[0, :, at(j)], v_ref[0, :, at(j)])

        def load(m, j):
            return src_ref[m, :, at(j)]

        def edges(m, j):
            return low_ref[m, :, at(j)], high_ref[m, :, at(j)]

        def emit(m, j, value):
            later = nu * t_ref[0, :, at(j)] + forcing_scale * w_ref[1, m, 0, :, at(j)].astype(F32)
            res_ref[m, :, at(j)] = value + later

        sweep(load, edges, coefs, emit, 2, lanes, rows)
        for value in range(4):

            @pl.when(k == value)
            def _(ref=outs[value]):
                ref[:, 0] = res_ref[...]

    def turn(value):
        def index(k, l, q, s):
            k = 3 - k
            return (0, jnp.where(k == value, l, jnp.where(k > value, 0, 1)), 0, 0)

        return index

    group = lambda k, l, q: 2 * q[8 + 3 - k] + l
    one = pl.BlockSpec((1, rows, nx), lambda k, l, q, s: (group(k, l, q), 0, 0))
    return pl.pallas_call(
        body,
        name="driven",
        out_shape=[jax.ShapeDtypeStruct((2, 2, rows, nx), F32)] * 4,
        grid_spec=pltpu.PrefetchScalarGridSpec(
            num_scalar_prefetch=2,
            grid=(4, 2),
            in_specs=[
                one,
                one,
                one,
                pl.BlockSpec(
                    (2, 2, 1, rows, nx), lambda k, l, q, s: (0, 0, group(k, l, q), 0, 0)
                ),
                table(below.shape),
                table(above.shape),
            ],
            out_specs=[pl.BlockSpec((2, 1, rows, nx), turn(value)) for value in range(4)],
            scratch_shapes=[
                pltpu.VMEM((2, rows, nx), F32),
                pltpu.VMEM((2, rows, nx), F32),
                pltpu.VMEM((2, 1, nx), F32),
                pltpu.VMEM((2, 1, nx), F32),
            ],
        ),
        compiler_params=params(16),
        cost_estimate=cost(40 * 2 * target.size, 28 * target.size),
    )(ids, scal, vx, vy, target, forcing, below, above)


def assemble(ids, moved, rests, tiles):
    _, _, rows, nx = moved.shape
    cols = nx // tiles
    per = 128 // cols

    def body(s, f0_ref, f1_ref, r0_ref, r1_ref, r2_ref, r3_ref, out_ref, sum_ref):
        k = pl.program_id(0)
        lane = lax.broadcasted_iota(jnp.int32, (rows, 128), 1)
        for value, ref in enumerate((r0_ref, r1_ref, r2_ref, r3_ref)):

            @pl.when(k == value)
            def _(ref=ref):
                sum_ref[0] = f0_ref[0] + ref[0]
                sum_ref[1] = f1_ref[0] + ref[1]

        for j in range(nx // 128):
            pieces = [sum_ref[m, l, :, at(j)] for m in range(2) for l in range(2)]
            for q in range(per):
                block = None
                for i in range(4):
                    shift = ((i - q) * cols) % 128
                    moved = pltpu.roll(pieces[i], shift, 1) if shift else pieces[i]
                    block = moved if block is None else jnp.where(lane >= i * cols, moved, block)
                out_ref[0, per * j + q] = block

    one = (1, 2, rows, nx)
    return pl.pallas_call(
        body,
        name="assemble",
        out_shape=jax.ShapeDtypeStruct((4, tiles, rows, 128), F32),
        grid_spec=pltpu.PrefetchScalarGridSpec(
            num_scalar_prefetch=1,
            grid=(4,),
            in_specs=[
                pl.BlockSpec(one, lambda k, s: (s[2 * k], 0, 0, 0)),
                pl.BlockSpec(one, lambda k, s: (s[2 * k + 1], 0, 0, 0)),
            ]
            + [table((2, 2, rows, nx))] * 4,
            out_specs=pl.BlockSpec((1, tiles, rows, 128), lambda k, s: (s[8 + k], 0, 0, 0)),
            scratch_shapes=[pltpu.VMEM((2, 2, rows, nx), F32)],
        ),
        compiler_params=params(20),
        cost_estimate=cost(moved.size, 16 * moved.size),
    )(ids, moved, moved, *rests)


def finish(depths, arrived, ny):
    pairs, tiles, rows, _ = arrived.shape
    levels = 2 * pairs
    group = 128 // rows
    blocks = 2 if tiles % (2 * group) == 0 else 1
    steps = tiles // (group * blocks)
    width = 128 * blocks
    scale = ny ** (-0.5)

    def body(s, a_ref, out_ref, sum_ref, carry):
        @pl.when(pl.program_id(0) == 0)
        def _():
            carry[...] = jnp.zeros_like(carry)

        r = lax.broadcasted_iota(jnp.int32, (128, 128), 0)
        c = lax.broadcasted_iota(jnp.int32, (128, 128), 1)
        tri = (r <= c).astype(jnp.bfloat16)
        for b in range(blocks):
            lanes = slice(128 * b, 128 * b + 128)
            total = None
            for lp in range(pairs):
                x = a_ref[lp, group * b : group * (b + 1)].reshape(128, 128).T
                x = x.reshape(2, 2, 32, 128)
                for k in range(2):
                    level = 2 * lp + k
                    out_ref[:, level, :, lanes] = x[:, k]
                    term = s[level] * x[:, k]
                    total = term if total is None else total + term
            total = total.reshape(64, 128)
            hi = total.astype(jnp.bfloat16)
            lo = (total - hi.astype(F32)).astype(jnp.bfloat16)
            run = jnp.dot(hi, tri, preferred_element_type=F32) + jnp.dot(
                lo, tri, preferred_element_type=F32
            )
            run = run + carry[...]
            carry[...] = jnp.broadcast_to(run[:, 127:128], (64, 128))
            sum_ref[:, :, lanes] = (run * scale).reshape(2, 32, 128)

    return pl.pallas_call(
        body,
        name="finish",
        out_shape=(
            jax.ShapeDtypeStruct((2, levels, 32, ny), F32),
            jax.ShapeDtypeStruct((2, 32, ny), F32),
        ),
        grid_spec=pltpu.PrefetchScalarGridSpec(
            num_scalar_prefetch=1,
            grid=(steps,),
            in_specs=[pl.BlockSpec((pairs, group * blocks, rows, 128), lambda i, s: (0, i, 0, 0))],
            out_specs=[
                pl.BlockSpec((2, levels, 32, width), lambda i, s: (0, 0, 0, i)),
                pl.BlockSpec((2, 32, width), lambda i, s: (0, 0, i)),
            ],
            scratch_shapes=[pltpu.VMEM((64, 128), F32)],
        ),
        compiler_params=params(16),
        cost_estimate=cost(20 * arrived.size, 12 * arrived.size),
    )(depths, arrived)


def on_device(
    ensemble,
    owners,
    velocity_x,
    northward_speed_ratio,
    target,
    forcing,
    diffusion,
    nudging,
    level_depths,
):
    tiles = lax.axis_size("tile")
    rows, _ = ensemble.shape[2:]
    group = lax.axis_index("particle")
    tile = lax.axis_index("tile")
    up = [(i, i + 1) for i in range(tiles - 1)]
    down = [(i + 1, i) for i in range(tiles - 1)]

    def trade(value, k):
        return lax.ppermute(value, "particle", [(i, i ^ k) for i in range(4)])

    parts = [ensemble, None, None, None]
    for k in (1, 3, 2):
        piece = lax.dynamic_slice_in_dim(ensemble, 2 * (group ^ k), 2, axis=1)
        parts[k] = trade(piece, k)

    others = group ^ jnp.arange(4, dtype=jnp.int32)
    wanted = jnp.take(owners.reshape(4, 2), others, axis=0).reshape(8)
    slots = 2 * ((wanted >> 1) ^ group) + (wanted & 1)
    ids = jnp.concatenate([slots, others]).astype(jnp.int32)
    edges_ok = jnp.stack([tile > 0, tile < tiles - 1]).astype(F32)
    scal = jnp.concatenate([diffusion, nudging, edges_ok])

    def exchange(pair):
        below = lax.ppermute(pair[0], "tile", up)
        above = lax.ppermute(pair[1], "tile", down)
        return below, above

    edges = pack_static(scal, velocity_x, northward_speed_ratio, target, forcing)
    static = exchange(edges)
    edges = pack_edges(ids, parts[:2], 60)
    near = exchange(edges)
    rests = driven(
        ids, scal, velocity_x, northward_speed_ratio, target, forcing, *static
    )
    rests = list(rests)
    for k in (3, 2, 1):
        rests[k] = trade(rests[k], k)
    moved = twice(
        ids, scal, parts[:2], velocity_x, northward_speed_ratio, near, static, None
    )
    edges = pack_edges(ids, parts[2:], 16)
    far = exchange(edges)
    moved = twice(
        ids, scal, parts[2:], velocity_x, northward_speed_ratio, far, static, moved
    )
    blocks = assemble(ids, moved, rests, tiles)
    arrived = lax.all_to_all(
        blocks.reshape(4 * tiles, rows, 128), ("particle", "tile"), 0, 0, tiled=True
    )
    return finish(level_depths, arrived.reshape(4, tiles, rows, 128), tiles * rows)


def solution(mesh):
    placed = (
        P("particle", None, "tile", None),
        P(),
        P(None, "tile", None),
        P(None, "tile", None),
        P(None, "tile", None),
        P(None, "particle", None, "tile", None),
        P(),
        P(),
        P(),
    )
    return jax.shard_map(
        on_device,
        mesh=mesh,
        in_specs=placed,
        out_specs=(P("particle", None, "tile", None), P("particle", "tile", None)),
        check_vma=False,
    )
```

time: 300 us -> 146 us (0.49)
  waiting for transfers between devices: 77 us -> 7.25 us
  local copies, waits for them, and re-layouts: 73 us -> 6.49 us
  other arithmetic: 51.2 us -> 1.5 us
  Pallas kernels: 0 us -> 30.8 us
  starting transfers between devices: 11.9 us -> 26 us
  between operations: 14.3 us -> 0.87 us
  matrix products: 11.9 us -> 0 us
  blocking collectives: 60.1 us -> 70.6 us
    all_gather x1 -> x0, waiting for transfers between devices: 64.7 us -> none  [on_device(): lax.all_gather(ensemble, 'particle', axis=0, tiled=True)]
    pallas_call x0 -> x8, Pallas kernels: none -> 30.8 us  [the longest x2 9.28 us: twice(): pl.pallas_call(body, name='twice', out_shape=jax.ShapeDtypeStruct((8, 2,...]
    all_to_all x3 -> x0, local copies, waits for them, and re-layouts: 26.5 us -> none  [on_device(): lax.all_to_all(turned, 'tile', split_axis=2, concat_axis=3, tiled=True)]
    unnamed x21 -> x20, local copies, waits for them, and re-layouts: 27.3 us -> 3.21 us
    another operation x2 -> x0, other arithmetic: 18.1 us -> none
    ppermute x4 -> x12, starting transfers between devices: 11.9 us -> 26 us  [the longest x3 12.3 us: exchange(): below = lax.ppermute(pair[0], 'tile', up)]
    transpose x1 -> x0, local copies, waits for them, and re-layouts: 11.9 us -> none  [on_device(): turned = jnp.transpose(prognostic_tracer, (0, 1, 3, 2))]
    dot_general x1 -> x0, matrix products: 11.9 us -> none  [select(): jnp.einsum('jk,klrx->jlrx', matches, arrived, precision=lax.Precision.HIG...]
  transfers between devices with their start and end apart: 5 -> 12, of which waited for: 5 -> 3; matrix products, arithmetic and copies ran while one was open for 2% -> 2% of each run, Pallas kernels for 0% -> 14%
where the time goes in v1:
time: 146 us; the launch traced here: 144 us
  blocking collectives  70.6 us (48%)
  Pallas kernels  30.8 us (21%)
  starting transfers between devices  26 us (18%)
  waiting for transfers between devices  7.25 us (5%)
  local copies, waits for them, and re-layouts  6.49 us (4%)
  other arithmetic  1.5 us (1%)
    all_to_all x1, blocking collectives, on_device(): lax.all_to_all(blocks.reshape(4 * tiles, rows, 128), ('particle', 'tile')...  70.6 us
    ppermute x3, starting transfers between devices, exchange(): below = lax.ppermute(pair[0], 'tile', up)  12.3 us
    pallas_call x2, Pallas kernels, twice(): pl.pallas_call(body, name='twice', out_shape=jax.ShapeDtypeStruct((8, 2,...  9.28 us
    ppermute x6, starting transfers between devices, trade(): return lax.ppermute(value, 'particle', [(i, i ^ k) for i in range(4)])  7.04 us
    ppermute x3, starting transfers between devices, exchange(): above = lax.ppermute(pair[1], 'tile', down)  6.75 us
    pallas_call x1, Pallas kernels, driven(): pl.pallas_call(body, name='driven', out_shape=[jax.ShapeDtypeStruct((2, 2...  6.25 us
    pallas_call x2, Pallas kernels, pack_edges(): pl.pallas_call(body, name='pack_edges', out_shape=(out, out), grid_spec=p...  4.52 us
    pallas_call x1, Pallas kernels, pack_static(): pl.pallas_call(body, name='pack_static', out_shape=(out, out), grid_spec=...  3.82 us
  transfers between devices with their start and end apart: 12, of which 3 were waited for; matrix products, arithmetic and copies ran while one was open for 2% of the time, Pallas kernels for 14%

profile of v1, /device:TPU:6, one launch (start us, length us, event | category | flops | bytes accessed | tf_op | source)
XLA Modules:
  0.0 143.5 jit_solution(6661369300217091414)
XLA Ops:
  0.6 0.1 add_convert_fusion
  0.7 1.3 pad_maximum_fusion.s
  2.0 3.8 %pack_static.1 = (f32[32,2048]{1,0:T(8,128)}, f32[32,2048]{1,0:T(8,128)}) custom-call(f32[18]{0:T(128)} %pad_maximum_fusion.s, f32[8,16,2048]{2,1,0:T(8,128)} %u_ref.7, f32[8,16,2048]{2,1,0:T(8,128)} %v_ref.7, f32[8,16,2048]{2,1,0:T(8,128)} %t_ref.3, bf16[2,2,8,16,2048]{4,3,2,1,0:T(8,128)(2,1)} %w_ref.3), custom_call_target="tpu_custom_call" | custom-call | bytes 4194304 | tf_op jit(solution)/shard_map/pack_static/pallas_call | solution.py:80
  5.8 4.0 %collective-permute-start.4 = (f32[32,2048]{1,0:T(8,128)}, f32[32,2048]{1,0:T(8,128)S(1)}, u32[]{:S(2)}, u32[]{:S(2)}) collective-permute-start(f32[32,2048]{1,0:T(8,128)} %get-tuple-element.14), channel_id=1, source_target_pairs={{0,1},{1,2},{2,3},{3,4},{4,5},{5,6},{6,7},{7,8},{8,9},{9,10},{10,1... | collective-permute-start | bytes 786440 | tf_op jit(solution)/shard_map/ppermute | solution.py:445
  9.8 2.1 %collective-permute-start.5 = (f32[32,2048]{1,0:T(8,128)}, f32[32,2048]{1,0:T(8,128)}, u32[]{:S(2)}, u32[]{:S(2)}) collective-permute-start(f32[32,2048]{1,0:T(8,128)} %get-tuple-element.15), channel_id=1, source_target_pairs={{1,0},{2,1},{3,2},{4,3},{5,4},{6,5},{7,6},{8,7},{9,8},{10,9},{11,1... | collective-permute-start | bytes 786440 | tf_op jit(solution)/shard_map/ppermute | solution.py:446
  12.0 2.6 %constant_dynamic-slice_fusion = (f32[2,2,16,2048]{3,2,1,0:T(8,128)}, f32[2,2,16,2048]{3,2,1,0:T(8,128)}, f32[2,2,16,2048]{3,2,1,0:T(8,128)}) fusion(f32[2,8,16,2048]{3,2,1,0:T(8,128)} %f0_ref.1, s32[]{:T(128)S(6)} %select_n.36, s32[]{:T(128)S(6)} %select_n.35, s32[]{:T(128)S(6)} %select_n.34), kind=kLoop, calls=%fused_computation.7 | loop fusion | bytes 3145740 | tf_op jit(solution)/shard_map/dynamic_slice | solution.py:434
  14.5 3.3 %collective-permute-start.1 = (f32[2,2,16,2048]{3,2,1,0:T(8,128)}, f32[2,2,16,2048]{3,2,1,0:T(8,128)}, u32[]{:S(2)}, u32[]{:S(2)}) collective-permute-start(f32[2,2,16,2048]{3,2,1,0:T(8,128)} %get-tuple-element.23), channel_id=1, source_target_pairs={{0,192},{64,128},{128,64},{192,0},{1,193},{65,129},{129,65},{193,1... | collective-permute-start | bytes 1572872 | tf_op jit(solution)/shard_map/ppermute | solution.py:430
  17.8 0.3 collective-permute-start
  18.2 0.1 reshape.47
  18.3 0.6 gather_fusion
  18.8 0.1 and_add_fusion
  18.9 0.1 reshape.50
  19.0 0.1 pad_add_fusion.s.q
  19.1 2.8 %collective-permute-done.5.sa_ref.above_ref = f32[32,2048]{1,0:T(8,128)} collective-permute-done((f32[32,2048]{1,0:T(8,128)}, f32[32,2048]{1,0:T(8,128)}, u32[]{:S(2)}, u32[]{:S(2)}) %collective-permute-start.5) | collective-permute-done | bytes 262176 | tf_op jit(solution)/shard_map/ppermute | solution.py:446
  21.9 1.6 %copy-done.3 = bf16[2,2,8,16,2048]{4,3,2,1,0:T(8,128)(2,1)S(1)} copy-done((bf16[2,2,8,16,2048]{4,3,2,1,0:T(8,128)(2,1)S(1)}, bf16[2,2,8,16,2048]{4,3,2,1,0:T(8,128)(2,1)}, u32[]{:S(2)}) %copy-start.3) | copy-done | bytes 2097176
  23.5 6.3 %driven.1 = (f32[2,2,16,2048]{3,2,1,0:T(8,128)S(1)}, f32[2,2,16,2048]{3,2,1,0:T(8,128)}, f32[2,2,16,2048]{3,2,1,0:T(8,128)}, f32[2,2,16,2048]{3,2,1,0:T(8,128)}) custom-call(s32[12]{0:T(128)S(1)} %pad_add_fusion.s.q, f32[18]{0:T(128)S(1)} %copy-done.7, f32[8,16,2048]{2,1,0:T(8,128)S(1)} %copy-done, f32[8,16,2048]{2,1,0:T(8,128)S(1)} %copy-done.1, ...), custom_call_target="tpu_custom_call" | custom-call | flops 20971520 | bytes 7340032 | tf_op jit(solution)/shard_map/driven/pallas_call | solution.py:275
  29.8 3.3 %collective-permute-start.10 = (f32[2,2,16,2048]{3,2,1,0:T(8,128)}, f32[2,2,16,2048]{3,2,1,0:T(8,128)S(1)}, u32[]{:S(2)}, u32[]{:S(2)}) collective-permute-start(f32[2,2,16,2048]{3,2,1,0:T(8,128)} %get-tuple-element.20), channel_id=1, source_target_pairs={{0,128},{64,192},{128,0},{192,64},{1,129},{65,193},{129,1},{193,65... | collective-permute-start | bytes 1572872 | tf_op jit(solution)/shard_map/ppermute | solution.py:430
  33.1 0.1 collective-permute-start.11
  33.2 2.7 %pack_edges.3 = (f32[16,2048]{1,0:T(8,128)}, f32[16,2048]{1,0:T(8,128)}) custom-call(s32[12]{0:T(128)} %copy-done.5, f32[2,8,16,2048]{3,2,1,0:T(8,128)} %f0_ref.1, f32[2,2,16,2048]{3,2,1,0:T(8,128)} %collective-permute-done.6.refs_1_.f1_ref), custom_call_target="tpu_custom_call" | custom-call | bytes 1048576 | tf_op jit(solution)/shard_map/pack_edges/pallas_call | solution.py:116
  35.9 3.0 %collective-permute-start.7 = (f32[16,2048]{1,0:T(8,128)}, f32[16,2048]{1,0:T(8,128)S(1)}, u32[]{:S(2)}, u32[]{:S(2)}) collective-permute-start(f32[16,2048]{1,0:T(8,128)} %get-tuple-element.16), channel_id=1, source_target_pairs={{0,1},{1,2},{2,3},{3,4},{4,5},{5,6},{6,7},{7,8},{8,9},{9,10},{10,1... | collective-permute-start | bytes 393224 | tf_op jit(solution)/shard_map/ppermute | solution.py:445
  38.9 3.6 %collective-permute-done.refs_0_.f0_ref = f32[2,2,16,2048]{3,2,1,0:T(8,128)} collective-permute-done((f32[2,2,16,2048]{3,2,1,0:T(8,128)}, f32[2,2,16,2048]{3,2,1,0:T(8,128)}, u32[]{:S(2)}, u32[]{:S(2)}) %collective-permute-start) | collective-permute-done | bytes 524320 | tf_op jit(solution)/shard_map/ppermute | solution.py:430
  42.5 2.7 %collective-permute-start.8 = (f32[16,2048]{1,0:T(8,128)}, f32[16,2048]{1,0:T(8,128)S(1)}, u32[]{:S(2)}, u32[]{:S(2)}) collective-permute-start(f32[16,2048]{1,0:T(8,128)} %get-tuple-element.17), channel_id=1, source_target_pairs={{1,0},{2,1},{3,2},{4,3},{5,4},{6,5},{7,6},{8,7},{9,8},{10,9},{11,1... | collective-permute-start | bytes 393224 | tf_op jit(solution)/shard_map/ppermute | solution.py:446
  45.2 1.8 %pack_edges.2 = (f32[16,2048]{1,0:T(8,128)S(1)}, f32[16,2048]{1,0:T(8,128)S(1)}) custom-call(s32[12]{0:T(128)S(1)} %copy-done.6, f32[2,2,16,2048]{3,2,1,0:T(8,128)} %collective-permute-done.refs_0_.f0_ref, f32[2,2,16,2048]{3,2,1,0:T(8,128)} %collective-permute-done.1.refs_1_.f1_ref), custom_call_target="tpu_custom_call" | custom-call | bytes 1048576 | tf_op jit(solution)/shard_map/pack_edges/pallas_call | solution.py:116
  47.1 5.2 %collective-permute-start.2 = (f32[16,2048]{1,0:T(8,128)S(1)}, f32[16,2048]{1,0:T(8,128)S(1)}, u32[]{:S(2)}, u32[]{:S(2)}) collective-permute-start(f32[16,2048]{1,0:T(8,128)S(1)} %get-tuple-element.12), channel_id=1, source_target_pairs={{0,1},{1,2},{2,3},{3,4},{4,5},{5,6},{6,7},{7,8},{8,9},{9,10},{10,1... | collective-permute-start | bytes 393224 | tf_op jit(solution)/shard_map/ppermute | solution.py:445
  52.3 1.9 %collective-permute-start.3 = (f32[16,2048]{1,0:T(8,128)S(1)}, f32[16,2048]{1,0:T(8,128)S(1)}, u32[]{:S(2)}, u32[]{:S(2)}) collective-permute-start(f32[16,2048]{1,0:T(8,128)S(1)} %get-tuple-element.13), channel_id=1, source_target_pairs={{1,0},{2,1},{3,2},{4,3},{5,4},{6,5},{7,6},{8,7},{9,8},{10,9},{11,1... | collective-permute-start | bytes 393224 | tf_op jit(solution)/shard_map/ppermute | solution.py:446
  54.3 1.6 %copy-done.2 = f32[2,8,16,2048]{3,2,1,0:T(8,128)S(1)} copy-done((f32[2,8,16,2048]{3,2,1,0:T(8,128)S(1)}, f32[2,8,16,2048]{3,2,1,0:T(8,128)}, u32[]{:S(2)}) %copy-start.2) | copy-done | bytes 2097176
  55.9 4.6 %twice.2.rest_0_ = f32[8,2,16,2048]{3,2,1,0:T(8,128)S(1)} custom-call(s32[12]{0:T(128)S(1)} %copy-done.6, f32[18]{0:T(128)S(1)} %copy-done.7, f32[2,8,16,2048]{3,2,1,0:T(8,128)S(1)} %copy-done.2, f32[2,2,16,2048]{3,2,1,0:T(8,128)} %collective-permute-done.6.refs_1_.f1_ref, f32[8,16,2048]{2,1,0:T(8,128)S(1)} %copy-done, f32[8,16,2048]{2,1,0:T(8,128)S(1)} %copy-done.1, ...), custom_call_target="tpu_custom_call" | custom-call | flops 15728640 | bytes 3145728 | tf_op jit(solution)/shard_map/twice/pallas_call | solution.py:207
  60.5 0.8 collective-permute-done.3.above_ref
  61.3 4.7 %twice.3.f0_ref.f1_ref = f32[8,2,16,2048]{3,2,1,0:T(8,128)S(1)} custom-call(s32[12]{0:T(128)S(1)} %copy-done.6, f32[18]{0:T(128)S(1)} %copy-done.7, f32[2,2,16,2048]{3,2,1,0:T(8,128)} %collective-permute-done.refs_0_.f0_ref, f32[2,2,16,2048]{3,2,1,0:T(8,128)} %collective-permute-done.1.refs_1_.f1_ref, ...), custom_call_target="tpu_custom_call", output_to_operand_aliasing={{}: (10, {})} | custom-call | flops 15728640 | bytes 3145728 | tf_op jit(solution)/shard_map/twice/pallas_call | solution.py:207
  66.0 3.8 %assemble.1 = f32[4,64,16,128]{3,2,1,0:T(8,128)S(1)} custom-call(s32[12]{0:T(128)S(1)} %copy-done.6, f32[8,2,16,2048]{3,2,1,0:T(8,128)S(1)} %twice.3.f0_ref.f1_ref, f32[8,2,16,2048]{3,2,1,0:T(8,128)S(1)} %twice.3.f0_ref.f1_ref, f32[2,2,16,2048]{3,2,1,0:T(8,128)S(1)} %get-tuple-element.18.r0_ref, f32[2,2,16,2048]{3,2,1,0:T(8,128)S(1)} %collective-permute-done.9.r1_ref, ...), custom_call_target="tpu_custom_call" | custom-call | flops 524288 | bytes 8388608 | tf_op jit(solution)/shard_map/assemble/pallas_call | solution.py:331
  69.8 70.6 %all_to_all.5 = f32[256,16,128]{2,1,0:T(8,128)S(1)} all-to-all(f32[256,16,128]{2,1,0:T(8,128)S(1)} %bitcast.7), channel_id=1, replica_groups=mesh['particle'=4,'tile'=64] {'particle','tile'}, dimensions={0} | all-to-all | bytes 4194304 | tf_op jit(solution)/shard_map/all_to_all | solution.py:468
  140.4 3.1 %finish.1 = (f32[2,8,32,1024]{3,2,1,0:T(8,128)}, f32[2,32,1024]{2,1,0:T(8,128)}) custom-call(f32[8]{0:T(128)S(1)} %copy-done.8, f32[4,64,16,128]{3,2,1,0:T(8,128)S(1)} %bitcast.6), custom_call_target="tpu_custom_call" | custom-call | flops 10485760 | bytes 6291456 | tf_op jit(solution)/shard_map/finish/pallas_call | solution.py:389
  (33 shorter events, 0.1 us)
Async XLA Ops:
  5.8 12.4 %copy-start.9 = (s32[8]{0:T(128)S(1)}, s32[8]{0:T(128)}, u32[]{:S(2)}) copy-start(s32[8]{0:T(128)} %param.10) | copy-start | bytes 100
  5.8 16.1 %copy-start = (f32[8,16,2048]{2,1,0:T(8,128)S(1)}, f32[8,16,2048]{2,1,0:T(8,128)}, u32[]{:S(2)}) copy-start(f32[8,16,2048]{2,1,0:T(8,128)} %u_ref.7) | copy-start | bytes 3145732
  5.8 16.1 %copy-start.1 = (f32[8,16,2048]{2,1,0:T(8,128)S(1)}, f32[8,16,2048]{2,1,0:T(8,128)}, u32[]{:S(2)}) copy-start(f32[8,16,2048]{2,1,0:T(8,128)} %v_ref.7) | copy-start | bytes 3145732
  5.8 16.1 %copy-start.4 = (f32[8,16,2048]{2,1,0:T(8,128)S(1)}, f32[8,16,2048]{2,1,0:T(8,128)}, u32[]{:S(2)}) copy-start(f32[8,16,2048]{2,1,0:T(8,128)} %t_ref.3) | copy-start | bytes 3145732
  5.8 16.1 %copy-start.7 = (f32[18]{0:T(128)S(1)}, f32[18]{0:T(128)}, u32[]{:S(2)}) copy-start(f32[18]{0:T(128)} %pad_maximum_fusion.s) | copy-start | bytes 220
  5.8 13.3 %collective-permute-start.4 = (f32[32,2048]{1,0:T(8,128)}, f32[32,2048]{1,0:T(8,128)S(1)}, u32[]{:S(2)}, u32[]{:S(2)}) collective-permute-start(f32[32,2048]{1,0:T(8,128)} %get-tuple-element.14), channel_id=1, source_target_pairs={{0,1},{1,2},{2,3},{3,4},{4,5},{5,6},{6,7},{7,8},{8,9},{9,10},{10,1... | collective-permute-start | bytes 786440 | tf_op jit(solution)/shard_map/ppermute | solution.py:445
  9.8 12.1 %collective-permute-start.5 = (f32[32,2048]{1,0:T(8,128)}, f32[32,2048]{1,0:T(8,128)}, u32[]{:S(2)}, u32[]{:S(2)}) collective-permute-start(f32[32,2048]{1,0:T(8,128)} %get-tuple-element.15), channel_id=1, source_target_pairs={{1,0},{2,1},{3,2},{4,3},{5,4},{6,5},{7,6},{8,7},{9,8},{10,9},{11,1... | collective-permute-start | bytes 786440 | tf_op jit(solution)/shard_map/ppermute | solution.py:446
  14.5 18.6 %collective-permute-start.6 = (f32[2,2,16,2048]{3,2,1,0:T(8,128)}, f32[2,2,16,2048]{3,2,1,0:T(8,128)}, u32[]{:S(2)}, u32[]{:S(2)}) collective-permute-start(f32[2,2,16,2048]{3,2,1,0:T(8,128)} %get-tuple-element.22), channel_id=1, source_target_pairs={{0,64},{64,0},{128,192},{192,128},{1,65},{65,1},{129,193},{193,129... | collective-permute-start | bytes 1572872 | tf_op jit(solution)/shard_map/ppermute | solution.py:430
  14.5 21.3 %collective-permute-start.1 = (f32[2,2,16,2048]{3,2,1,0:T(8,128)}, f32[2,2,16,2048]{3,2,1,0:T(8,128)}, u32[]{:S(2)}, u32[]{:S(2)}) collective-permute-start(f32[2,2,16,2048]{3,2,1,0:T(8,128)} %get-tuple-element.23), channel_id=1, source_target_pairs={{0,192},{64,128},{128,64},{192,0},{1,193},{65,129},{129,65},{193,1... | collective-permute-start | bytes 1572872 | tf_op jit(solution)/shard_map/ppermute | solution.py:430
  17.8 24.7 %collective-permute-start = (f32[2,2,16,2048]{3,2,1,0:T(8,128)}, f32[2,2,16,2048]{3,2,1,0:T(8,128)}, u32[]{:S(2)}, u32[]{:S(2)}) collective-permute-start(f32[2,2,16,2048]{3,2,1,0:T(8,128)} %get-tuple-element.24), channel_id=1, source_target_pairs={{0,128},{64,192},{128,0},{192,64},{1,129},{65,193},{129,1},{193,65... | collective-permute-start | bytes 1572872 | tf_op jit(solution)/shard_map/ppermute | solution.py:430
  19.1 10.7 %copy-start.5 = (s32[12]{0:T(128)}, s32[12]{0:T(128)S(1)}, u32[]{:S(2)}) copy-start(s32[12]{0:T(128)S(1)} %pad_add_fusion.s.q) | copy-start | bytes 148
  21.9 1.6 %copy-start.3 = (bf16[2,2,8,16,2048]{4,3,2,1,0:T(8,128)(2,1)S(1)}, bf16[2,2,8,16,2048]{4,3,2,1,0:T(8,128)(2,1)}, u32[]{:S(2)}) copy-start(bf16[2,2,8,16,2048]{4,3,2,1,0:T(8,128)(2,1)} %w_ref.3) | copy-start | bytes 6291460
  29.8 15.4 %copy-start.6 = (s32[12]{0:T(128)S(1)}, s32[12]{0:T(128)}, u32[]{:S(2)}) copy-start(s32[12]{0:T(128)} %copy-done.5) | copy-start | bytes 148
  29.8 36.2 %collective-permute-start.9 = (f32[2,2,16,2048]{3,2,1,0:T(8,128)}, f32[2,2,16,2048]{3,2,1,0:T(8,128)S(1)}, u32[]{:S(2)}, u32[]{:S(2)}) collective-permute-start(f32[2,2,16,2048]{3,2,1,0:T(8,128)} %get-tuple-element.19), channel_id=1, source_target_pairs={{0,64},{64,0},{128,192},{192,128},{1,65},{65,1},{129,193},{193,129... | collective-permute-start | bytes 1572872 | tf_op jit(solution)/shard_map/ppermute | solution.py:430
  29.8 36.2 %collective-permute-start.10 = (f32[2,2,16,2048]{3,2,1,0:T(8,128)}, f32[2,2,16,2048]{3,2,1,0:T(8,128)S(1)}, u32[]{:S(2)}, u32[]{:S(2)}) collective-permute-start(f32[2,2,16,2048]{3,2,1,0:T(8,128)} %get-tuple-element.20), channel_id=1, source_target_pairs={{0,128},{64,192},{128,0},{192,64},{1,129},{65,193},{129,1},{193,65... | collective-permute-start | bytes 1572872 | tf_op jit(solution)/shard_map/ppermute | solution.py:430
  33.1 32.9 %collective-permute-start.11 = (f32[2,2,16,2048]{3,2,1,0:T(8,128)}, f32[2,2,16,2048]{3,2,1,0:T(8,128)}, u32[]{:S(2)}, u32[]{:S(2)}) collective-permute-start(f32[2,2,16,2048]{3,2,1,0:T(8,128)} %get-tuple-element.21), channel_id=1, source_target_pairs={{0,192},{64,128},{128,64},{192,0},{1,193},{65,129},{129,65},{193,1... | collective-permute-start | bytes 1572872 | tf_op jit(solution)/shard_map/ppermute | solution.py:430
  35.9 11.2 %collective-permute-start.7 = (f32[16,2048]{1,0:T(8,128)}, f32[16,2048]{1,0:T(8,128)S(1)}, u32[]{:S(2)}, u32[]{:S(2)}) collective-permute-start(f32[16,2048]{1,0:T(8,128)} %get-tuple-element.16), channel_id=1, source_target_pairs={{0,1},{1,2},{2,3},{3,4},{4,5},{5,6},{6,7},{7,8},{8,9},{9,10},{10,1... | collective-permute-start | bytes 393224 | tf_op jit(solution)/shard_map/ppermute | solution.py:445
  42.5 9.8 %collective-permute-start.8 = (f32[16,2048]{1,0:T(8,128)}, f32[16,2048]{1,0:T(8,128)S(1)}, u32[]{:S(2)}, u32[]{:S(2)}) collective-permute-start(f32[16,2048]{1,0:T(8,128)} %get-tuple-element.17), channel_id=1, source_target_pairs={{1,0},{2,1},{3,2},{4,3},{5,4},{6,5},{7,6},{8,7},{9,8},{10,9},{11,1... | collective-permute-start | bytes 393224 | tf_op jit(solution)/shard_map/ppermute | solution.py:446
  47.1 13.4 %collective-permute-start.2 = (f32[16,2048]{1,0:T(8,128)S(1)}, f32[16,2048]{1,0:T(8,128)S(1)}, u32[]{:S(2)}, u32[]{:S(2)}) collective-permute-start(f32[16,2048]{1,0:T(8,128)S(1)} %get-tuple-element.12), channel_id=1, source_target_pairs={{0,1},{1,2},{2,3},{3,4},{4,5},{5,6},{6,7},{7,8},{8,9},{9,10},{10,1... | collective-permute-start | bytes 393224 | tf_op jit(solution)/shard_map/ppermute | solution.py:445
  52.3 9.0 %collective-permute-start.3 = (f32[16,2048]{1,0:T(8,128)S(1)}, f32[16,2048]{1,0:T(8,128)S(1)}, u32[]{:S(2)}, u32[]{:S(2)}) collective-permute-start(f32[16,2048]{1,0:T(8,128)S(1)} %get-tuple-element.13), channel_id=1, source_target_pairs={{1,0},{2,1},{3,2},{4,3},{5,4},{6,5},{7,6},{8,7},{9,8},{10,9},{11,1... | collective-permute-start | bytes 393224 | tf_op jit(solution)/shard_map/ppermute | solution.py:446
  54.3 1.6 %copy-start.2 = (f32[2,8,16,2048]{3,2,1,0:T(8,128)S(1)}, f32[2,8,16,2048]{3,2,1,0:T(8,128)}, u32[]{:S(2)}) copy-start(f32[2,8,16,2048]{3,2,1,0:T(8,128)} %f0_ref.1) | copy-start | bytes 6291460
  69.8 70.6 %copy-start.8 = (f32[8]{0:T(128)S(1)}, f32[8]{0:T(128)}, u32[]{:S(2)}) copy-start(f32[8]{0:T(128)} %s.1) | copy-start | bytes 100

commit v2 on v1

--- a/solution.py
+++ b/solution.py
@@ -71,7 +71,7 @@
                 ref[levels + l : levels + l + 1] = v_ref[l, r : r + 1]
                 nt = s[8 + l] * t_ref[l, r : r + 1]
                 for m in range(2):
-                    w = w_ref[0, m, l].astype(F32)[r : r + 1]
+                    w = w_ref[0, m, l, r : r + 1].astype(F32)
                     i = (2 + m) * levels + l
                     ref[i : i + 1] = nt + forcing_scale * w
 
@@ -87,7 +87,7 @@
             in_specs=[table(vx.shape)] * 3 + [table((1,) + forcing.shape[1:])],
             out_specs=[table(shape)] * 2,
         ),
-        compiler_params=params(60),
+        compiler_params=params(16),
         cost_estimate=cost(0, 16 * target.size),
     )(scal, vx, vy, target, forcing)
 
@@ -233,7 +233,7 @@
     def body(q, s, u_ref, v_ref, t_ref, w_ref, below_ref, above_ref, *rest):
         outs, (src_ref, res_ref, low_ref, high_ref) = rest[:4], rest[4:]
         k, l = 3 - pl.program_id(0), pl.program_id(1)
-        level = 2 * q[8 + k] + l
+        level = 2 * (q[8] ^ k) + l
         d, nu = s[level], s[8 + level]
         for m in range(2):
             low_ref[m] = below_ref[pl.ds((2 + m) * level_count + level, 1), :]
@@ -270,7 +270,7 @@
 
         return index
 
-    group = lambda k, l, q: 2 * q[8 + 3 - k] + l
+    group = lambda k, l, q: 2 * (q[8] ^ (3 - k)) + l
     one = pl.BlockSpec((1, rows, nx), lambda k, l, q, s: (group(k, l, q), 0, 0))
     return pl.pallas_call(
         body,
@@ -302,15 +302,21 @@
     )(ids, scal, vx, vy, target, forcing, below, above)
 
 
-def assemble(ids, moved, rests, tiles):
+def slot(ids, k, m):
+    member = ids[2 * (ids[8] ^ k) + m]
+    return 2 * ((member >> 1) ^ ids[8]) + (member & 1)
+
+
+def assemble(ids, moved, rests, tiles, base, before):
     _, _, rows, nx = moved.shape
     cols = nx // tiles
     per = 128 // cols
 
-    def body(s, f0_ref, f1_ref, r0_ref, r1_ref, r2_ref, r3_ref, out_ref, sum_ref):
+    def body(s, f0_ref, f1_ref, r0_ref, r1_ref, *rest):
+        out_ref, sum_ref = rest[-2:]
         k = pl.program_id(0)
         lane = lax.broadcasted_iota(jnp.int32, (rows, 128), 1)
-        for value, ref in enumerate((r0_ref, r1_ref, r2_ref, r3_ref)):
+        for value, ref in enumerate((r0_ref, r1_ref)):
 
             @pl.when(k == value)
             def _(ref=ref):
@@ -328,24 +334,31 @@
                 out_ref[0, per * j + q] = block
 
     one = (1, 2, rows, nx)
+    in_specs = [
+        pl.BlockSpec(one, lambda k, s: (slot(s, base + k, 0), 0, 0, 0)),
+        pl.BlockSpec(one, lambda k, s: (slot(s, base + k, 1), 0, 0, 0)),
+    ] + [table((2, 2, rows, nx))] * 2
+    args = [ids, moved, moved, *rests]
+    aliases = {}
+    if before is not None:
+        aliases = {len(args): 0}
+        in_specs.append(pl.BlockSpec(memory_space=pl.ANY))
+        args.append(before)
     return pl.pallas_call(
         body,
         name="assemble",
         out_shape=jax.ShapeDtypeStruct((4, tiles, rows, 128), F32),
         grid_spec=pltpu.PrefetchScalarGridSpec(
             num_scalar_prefetch=1,
-            grid=(4,),
-            in_specs=[
-                pl.BlockSpec(one, lambda k, s: (s[2 * k], 0, 0, 0)),
-                pl.BlockSpec(one, lambda k, s: (s[2 * k + 1], 0, 0, 0)),
-            ]
-            + [table((2, 2, rows, nx))] * 4,
-            out_specs=pl.BlockSpec((1, tiles, rows, 128), lambda k, s: (s[8 + k], 0, 0, 0)),
+            grid=(2,),
+            in_specs=in_specs,
+            out_specs=pl.BlockSpec((1, tiles, rows, 128), lambda k, s: (s[8] ^ (base + k), 0, 0, 0)),
             scratch_shapes=[pltpu.VMEM((2, 2, rows, nx), F32)],
         ),
+        input_output_aliases=aliases,
         compiler_params=params(20),
-        cost_estimate=cost(moved.size, 16 * moved.size),
-    )(ids, moved, moved, *rests)
+        cost_estimate=cost(moved.size, 8 * moved.size),
+    )(*args)
 
 
 def finish(depths, arrived, ny):
@@ -429,15 +442,12 @@
     def trade(value, k):
         return lax.ppermute(value, "particle", [(i, i ^ k) for i in range(4)])
 
-    parts = [ensemble, None, None, None]
-    for k in (1, 3, 2):
-        piece = lax.dynamic_slice_in_dim(ensemble, 2 * (group ^ k), 2, axis=1)
-        parts[k] = trade(piece, k)
-
-    others = group ^ jnp.arange(4, dtype=jnp.int32)
-    wanted = jnp.take(owners.reshape(4, 2), others, axis=0).reshape(8)
-    slots = 2 * ((wanted >> 1) ^ group) + (wanted & 1)
-    ids = jnp.concatenate([slots, others]).astype(jnp.int32)
+    pieces = [lax.dynamic_slice_in_dim(ensemble, 2 * (group ^ k), 2, axis=1) for k in range(4)]
+    parts = [pieces[0], None, None, None]
+    for k in (3, 2, 1):
+        parts[k] = trade(pieces[k], k)
+
+    ids = jnp.concatenate([owners, group[None].astype(jnp.int32)])
     edges_ok = jnp.stack([tile > 0, tile < tiles - 1]).astype(F32)
     scal = jnp.concatenate([diffusion, nudging, edges_ok])
 
@@ -448,7 +458,7 @@
 
     edges = pack_static(scal, velocity_x, northward_speed_ratio, target, forcing)
     static = exchange(edges)
-    edges = pack_edges(ids, parts[:2], 60)
+    edges = pack_edges(ids, parts[:2], 16)
     near = exchange(edges)
     rests = driven(
         ids, scal, velocity_x, northward_speed_ratio, target, forcing, *static
@@ -456,15 +466,16 @@
     rests = list(rests)
     for k in (3, 2, 1):
         rests[k] = trade(rests[k], k)
+    edges = pack_edges(ids, parts[2:], 16)
+    far = exchange(edges)
     moved = twice(
         ids, scal, parts[:2], velocity_x, northward_speed_ratio, near, static, None
     )
-    edges = pack_edges(ids, parts[2:], 16)
-    far = exchange(edges)
     moved = twice(
         ids, scal, parts[2:], velocity_x, northward_speed_ratio, far, static, moved
     )
-    blocks = assemble(ids, moved, rests, tiles)
+    blocks = assemble(ids, moved, rests[:2], tiles, 0, None)
+    blocks = assemble(ids, moved, rests[2:], tiles, 2, blocks)
     arrived = lax.all_to_all(
         blocks.reshape(4 * tiles, rows, 128), ("particle", "tile"), 0, 0, tiled=True
     )

time: 146 us -> 145 us (level)
  Pallas kernels: 30.8 us -> 18.8 us
  waiting for transfers between devices: 7.25 us -> 17 us
  blocking collectives: 70.6 us -> 74.2 us
    ppermute x3, waiting for transfers between devices: 3.66 us -> 9.8 us  [exchange(): above = lax.ppermute(pair[1], 'tile', down)]
    all_to_all x1, blocking collectives: 70.6 us -> 74.2 us  [on_device(): lax.all_to_all(blocks.reshape(4 * tiles, rows, 128), ('particle', 'tile')...]
    pallas_call x2, Pallas kernels: 4.52 us -> 1.3 us  [pack_edges(): pl.pallas_call(body, name='pack_edges', out_shape=(out, out), grid_spec=p...]
    pallas_call x1, Pallas kernels: 3.82 us -> 0.82 us  [pack_static(): pl.pallas_call(body, name='pack_static', out_shape=(out, out), grid_spec=...]
    pallas_call x2, Pallas kernels: 9.28 us -> 6.6 us  [twice(): pl.pallas_call(body, name='twice', out_shape=jax.ShapeDtypeStruct((8, 2,...]
    pallas_call x1, Pallas kernels: 6.25 us -> 3.7 us  [driven(): pl.pallas_call(body, name='driven', out_shape=[jax.ShapeDtypeStruct((2, 2...]
    ppermute x6, waiting for transfers between devices: 3.58 us -> 5.89 us  [trade(): return lax.ppermute(value, 'particle', [(i, i ^ k) for i in range(4)])]
    pallas_call x1 -> x2, Pallas kernels: 3.8 us -> 3.3 us  [assemble(): pl.pallas_call(body, name='assemble', out_shape=jax.ShapeDtypeStruct((4,...]
  transfers between devices with their start and end apart: 12 -> 12, of which waited for: 3 -> 5; matrix products, arithmetic and copies ran while one was open for 2% -> 0% of each run, Pallas kernels for 14% -> 10%
where the time goes in v2:
time: 145 us; the launch traced here: 143 us
  blocking collectives  74.2 us (51%)
  starting transfers between devices  25.9 us (18%)
  Pallas kernels  18.8 us (13%)
  waiting for transfers between devices  17 us (12%)
  local copies, waits for them, and re-layouts  5.73 us (4%)
    all_to_all x1, blocking collectives, on_device(): lax.all_to_all(blocks.reshape(4 * tiles, rows, 128), ('particle', 'tile')...  74.2 us
    ppermute x3, starting transfers between devices, exchange(): below = lax.ppermute(pair[0], 'tile', up)  12.3 us
    ppermute x3, waiting for transfers between devices, exchange(): above = lax.ppermute(pair[1], 'tile', down)  9.8 us
    ppermute x6, starting transfers between devices, trade(): return lax.ppermute(value, 'particle', [(i, i ^ k) for i in range(4)])  6.84 us
    ppermute x3, starting transfers between devices, exchange(): above = lax.ppermute(pair[1], 'tile', down)  6.74 us
    pallas_call x2, Pallas kernels, twice(): pl.pallas_call(body, name='twice', out_shape=jax.ShapeDtypeStruct((8, 2,...  6.6 us
    ppermute x6, waiting for transfers between devices, trade(): return lax.ppermute(value, 'particle', [(i, i ^ k) for i in range(4)])  5.89 us
    pallas_call x1, Pallas kernels, driven(): pl.pallas_call(body, name='driven', out_shape=[jax.ShapeDtypeStruct((2, 2...  3.7 us
  transfers between devices with their start and end apart: 12, of which 5 were waited for; matrix products, arithmetic and copies ran while one was open for 0% of the time, Pallas kernels for 10%

profile of v2, /device:TPU:6, one launch (start us, length us, event | category | flops | bytes accessed | tf_op | source)
XLA Modules:
  0.0 142.8 jit_solution(2598454715935057624)
XLA Ops:
  0.7 2.9 %constant_dynamic-slice_fusion = (f32[2,2,16,2048]{3,2,1,0:T(8,128)}, f32[2,2,16,2048]{3,2,1,0:T(8,128)}, f32[2,2,16,2048]{3,2,1,0:T(8,128)}, f32[2,2,16,2048]{3,2,1,0:T(8,128)S(1)}) fusion(f32[2,8,16,2048]{3,2,1,0:T(8,128)} %param.9, s32[]{:T(128)S(6)} %select_n.15, s32[]{:T(128)S(6)} %select_n.13, s32[]{:T(128)S(6)} %select_n.12, s32[]{:T(128)S(6)} %select_n.14), kind=kLoop, calls=%fused_computation.1 | loop fusion | bytes 4194320 | tf_op jit(solution)/shard_map/dynamic_slice | solution.py:445
  3.6 0.1 add_convert_fusion
  3.7 0.1 pad_maximum_fusion.s
  3.7 1.6 %copy-done.2 = bf16[2,2,8,16,2048]{4,3,2,1,0:T(8,128)(2,1)S(1)} copy-done((bf16[2,2,8,16,2048]{4,3,2,1,0:T(8,128)(2,1)S(1)}, bf16[2,2,8,16,2048]{4,3,2,1,0:T(8,128)(2,1)}, u32[]{:S(2)}) %copy-start.2) | copy-done | bytes 2097176
  5.3 1.2 copy-done.4
  6.6 0.8 pack_static.1
  7.4 3.9 %collective-permute-start.4 = (f32[32,2048]{1,0:T(8,128)S(1)}, f32[32,2048]{1,0:T(8,128)S(1)}, u32[]{:S(2)}, u32[]{:S(2)}) collective-permute-start(f32[32,2048]{1,0:T(8,128)S(1)} %get-tuple-element.14), channel_id=1, source_target_pairs={{0,1},{1,2},{2,3},{3,4},{4,5},{5,6},{6,7},{7,8},{8,9},{9,10},{10,1... | collective-permute-start | bytes 786440 | tf_op jit(solution)/shard_map/ppermute | solution.py:455
  11.3 2.1 %collective-permute-start.5 = (f32[32,2048]{1,0:T(8,128)S(1)}, f32[32,2048]{1,0:T(8,128)S(1)}, u32[]{:S(2)}, u32[]{:S(2)}) collective-permute-start(f32[32,2048]{1,0:T(8,128)S(1)} %get-tuple-element.15), channel_id=1, source_target_pairs={{1,0},{2,1},{3,2},{4,3},{5,4},{6,5},{7,6},{8,7},{9,8},{10,9},{11,1... | collective-permute-start | bytes 786440 | tf_op jit(solution)/shard_map/ppermute | solution.py:456
  13.4 2.9 %collective-permute-start.1 = (f32[2,2,16,2048]{3,2,1,0:T(8,128)S(1)}, f32[2,2,16,2048]{3,2,1,0:T(8,128)S(1)}, u32[]{:S(2)}, u32[]{:S(2)}) collective-permute-start(f32[2,2,16,2048]{3,2,1,0:T(8,128)S(1)} %copy-done.8), channel_id=1, source_target_pairs={{0,192},{64,128},{128,64},{192,0},{1,193},{65,129},{129,65},{193,1... | collective-permute-start | bytes 1572872 | tf_op jit(solution)/shard_map/ppermute | solution.py:443
  16.3 0.5 collective-permute-start
  16.8 0.1 pad_add_fusion.s.q
  16.9 1.3 collective-permute-done.4.sb_ref.below_ref
  18.2 5.6 %collective-permute-done.5.sa_ref.above_ref = f32[32,2048]{1,0:T(8,128)S(1)} collective-permute-done((f32[32,2048]{1,0:T(8,128)S(1)}, f32[32,2048]{1,0:T(8,128)S(1)}, u32[]{:S(2)}, u32[]{:S(2)}) %collective-permute-start.5) | collective-permute-done | bytes 262176 | tf_op jit(solution)/shard_map/ppermute | solution.py:456
  23.7 3.7 %driven.1 = (f32[2,2,16,2048]{3,2,1,0:T(8,128)S(1)}, f32[2,2,16,2048]{3,2,1,0:T(8,128)S(1)}, f32[2,2,16,2048]{3,2,1,0:T(8,128)S(1)}, f32[2,2,16,2048]{3,2,1,0:T(8,128)S(1)}) custom-call(s32[9]{0:T(128)S(1)} %pad_add_fusion.s.q, f32[18]{0:T(128)S(1)} %pad_maximum_fusion.s, f32[8,16,2048]{2,1,0:T(8,128)S(1)} %copy-done, f32[8,16,2048]{2,1,0:T(8,128)S(1)} %copy-done.1, ...), custom_call_target="tpu_custom_call" | custom-call | flops 20971520 | bytes 7340032 | tf_op jit(solution)/shard_map/driven/pallas_call | solution.py:275
  27.4 0.1 collective-permute-start.11
  27.5 3.3 %collective-permute-start.9 = (f32[2,2,16,2048]{3,2,1,0:T(8,128)S(1)}, f32[2,2,16,2048]{3,2,1,0:T(8,128)S(1)}, u32[]{:S(2)}, u32[]{:S(2)}) collective-permute-start(f32[2,2,16,2048]{3,2,1,0:T(8,128)S(1)} %get-tuple-element.18), channel_id=1, source_target_pairs={{0,128},{64,192},{128,0},{192,64},{1,129},{65,193},{129,1},{193,65... | collective-permute-start | bytes 1572872 | tf_op jit(solution)/shard_map/ppermute | solution.py:443
  30.8 0.1 collective-permute-start.10
  30.9 0.6 pack_edges.3
  31.6 3.3 %collective-permute-start.7 = (f32[16,2048]{1,0:T(8,128)S(1)}, f32[16,2048]{1,0:T(8,128)S(1)}, u32[]{:S(2)}, u32[]{:S(2)}) collective-permute-start(f32[16,2048]{1,0:T(8,128)S(1)} %get-tuple-element.16), channel_id=1, source_target_pairs={{0,1},{1,2},{2,3},{3,4},{4,5},{5,6},{6,7},{7,8},{8,9},{9,10},{10,1... | collective-permute-start | bytes 393224 | tf_op jit(solution)/shard_map/ppermute | solution.py:455
  34.8 5.9 %collective-permute-done.refs_0_.f0_ref = f32[2,2,16,2048]{3,2,1,0:T(8,128)S(1)} collective-permute-done((f32[2,2,16,2048]{3,2,1,0:T(8,128)S(1)}, f32[2,2,16,2048]{3,2,1,0:T(8,128)S(1)}, u32[]{:S(2)}, u32[]{:S(2)}) %collective-permute-start) | collective-permute-done | bytes 524320 | tf_op jit(solution)/shard_map/ppermute | solution.py:443
  40.7 2.7 %collective-permute-start.8 = (f32[16,2048]{1,0:T(8,128)S(1)}, f32[16,2048]{1,0:T(8,128)S(1)}, u32[]{:S(2)}, u32[]{:S(2)}) collective-permute-start(f32[16,2048]{1,0:T(8,128)S(1)} %get-tuple-element.17), channel_id=1, source_target_pairs={{1,0},{2,1},{3,2},{4,3},{5,4},{6,5},{7,6},{8,7},{9,8},{10,9},{11,1... | collective-permute-start | bytes 393224 | tf_op jit(solution)/shard_map/ppermute | solution.py:456
  43.4 0.6 pack_edges.2
  44.1 5.2 %collective-permute-start.2 = (f32[16,2048]{1,0:T(8,128)S(1)}, f32[16,2048]{1,0:T(8,128)S(1)}, u32[]{:S(2)}, u32[]{:S(2)}) collective-permute-start(f32[16,2048]{1,0:T(8,128)S(1)} %get-tuple-element.12), channel_id=1, source_target_pairs={{0,1},{1,2},{2,3},{3,4},{4,5},{5,6},{6,7},{7,8},{8,9},{9,10},{10,1... | collective-permute-start | bytes 393224 | tf_op jit(solution)/shard_map/ppermute | solution.py:455
  49.3 0.5 collective-permute-done.8.above_ref
  49.8 1.9 %collective-permute-start.3 = (f32[16,2048]{1,0:T(8,128)S(1)}, f32[16,2048]{1,0:T(8,128)S(1)}, u32[]{:S(2)}, u32[]{:S(2)}) collective-permute-start(f32[16,2048]{1,0:T(8,128)S(1)} %get-tuple-element.13), channel_id=1, source_target_pairs={{1,0},{2,1},{3,2},{4,3},{5,4},{6,5},{7,6},{8,7},{9,8},{10,9},{11,1... | collective-permute-start | bytes 393224 | tf_op jit(solution)/shard_map/ppermute | solution.py:456
  51.7 3.3 %twice.2.rest_0_ = f32[8,2,16,2048]{3,2,1,0:T(8,128)S(1)} custom-call(s32[9]{0:T(128)S(1)} %pad_add_fusion.s.q, f32[18]{0:T(128)S(1)} %pad_maximum_fusion.s, f32[2,2,16,2048]{3,2,1,0:T(8,128)S(1)} %get-tuple-element.25.refs_0_.f0_ref, f32[2,2,16,2048]{3,2,1,0:T(8,128)S(1)} %collective-permute-done.6.refs_1_.f1_ref, f32[8,16,2048]{2,1,0:T(8,128)S(1)} %copy-done, ...), custom_call_target="tpu_custom_call" | custom-call | flops 15728640 | bytes 3145728 | tf_op jit(solution)/shard_map/twice/pallas_call | solution.py:207
  55.1 3.7 %collective-permute-done.3.above_ref = f32[16,2048]{1,0:T(8,128)S(1)} collective-permute-done((f32[16,2048]{1,0:T(8,128)S(1)}, f32[16,2048]{1,0:T(8,128)S(1)}, u32[]{:S(2)}, u32[]{:S(2)}) %collective-permute-start.3) | collective-permute-done | bytes 131104 | tf_op jit(solution)/shard_map/ppermute | solution.py:456
  58.8 3.3 %twice.3.f0_ref.f1_ref = f32[8,2,16,2048]{3,2,1,0:T(8,128)S(1)} custom-call(s32[9]{0:T(128)S(1)} %pad_add_fusion.s.q, f32[18]{0:T(128)S(1)} %pad_maximum_fusion.s, f32[2,2,16,2048]{3,2,1,0:T(8,128)S(1)} %collective-permute-done.refs_0_.f0_ref, f32[2,2,16,2048]{3,2,1,0:T(8,128)S(1)} %collective-permute-done.1.refs_1_.f1_ref, ...), custom_call_target="tpu_custom_call", output_to_operand_aliasing={{}: (10, {})} | custom-call | flops 15728640 | bytes 3145728 | tf_op jit(solution)/shard_map/twice/pallas_call | solution.py:207
  62.1 1.7 %assemble.2.rest_0_ = f32[4,64,16,128]{3,2,1,0:T(8,128)S(1)} custom-call(s32[9]{0:T(128)S(1)} %pad_add_fusion.s.q, f32[8,2,16,2048]{3,2,1,0:T(8,128)S(1)} %twice.3.f0_ref.f1_ref, f32[8,2,16,2048]{3,2,1,0:T(8,128)S(1)} %twice.3.f0_ref.f1_ref, f32[2,2,16,2048]{3,2,1,0:T(8,128)S(1)} %get-tuple-element.20.r0_ref, ...), custom_call_target="tpu_custom_call" | custom-call | flops 524288 | bytes 4194304 | tf_op jit(solution)/shard_map/assemble/pallas_call | solution.py:347
  63.8 1.7 %assemble.3 = f32[4,64,16,128]{3,2,1,0:T(8,128)S(1)} custom-call(s32[9]{0:T(128)S(1)} %pad_add_fusion.s.q, f32[8,2,16,2048]{3,2,1,0:T(8,128)S(1)} %twice.3.f0_ref.f1_ref, f32[8,2,16,2048]{3,2,1,0:T(8,128)S(1)} %twice.3.f0_ref.f1_ref, f32[2,2,16,2048]{3,2,1,0:T(8,128)S(1)} %collective-permute-done.9.r0_ref, ...), custom_call_target="tpu_custom_call", output_to_operand_aliasing={{}: (5, {})} | custom-call | flops 524288 | bytes 4194304 | tf_op jit(solution)/shard_map/assemble/pallas_call | solution.py:347
  65.4 74.2 %all_to_all.5 = f32[256,16,128]{2,1,0:T(8,128)S(1)} all-to-all(f32[256,16,128]{2,1,0:T(8,128)S(1)} %bitcast.5), channel_id=1, replica_groups=mesh['particle'=4,'tile'=64] {'particle','tile'}, dimensions={0} | all-to-all | bytes 4194304 | tf_op jit(solution)/shard_map/all_to_all | solution.py:479
  139.7 3.1 %finish.1 = (f32[2,8,32,1024]{3,2,1,0:T(8,128)}, f32[2,32,1024]{2,1,0:T(8,128)}) custom-call(f32[8]{0:T(128)S(1)} %copy-done.6, f32[4,64,16,128]{3,2,1,0:T(8,128)S(1)} %bitcast.6), custom_call_target="tpu_custom_call" | custom-call | flops 10485760 | bytes 6291456 | tf_op jit(solution)/shard_map/finish/pallas_call | solution.py:402
  (30 shorter events, 0.1 us)
Async XLA Ops:
  0.7 3.0 %copy-start.9 = (f32[8]{0:T(128)S(1)}, f32[8]{0:T(128)}, u32[]{:S(2)}) copy-start(f32[8]{0:T(128)} %param.16) | copy-start | bytes 100
  0.7 3.0 %copy-start.10 = (f32[8]{0:T(128)S(1)}, f32[8]{0:T(128)}, u32[]{:S(2)}) copy-start(f32[8]{0:T(128)} %param.15) | copy-start | bytes 100
  0.7 3.1 %copy-start = (f32[8,16,2048]{2,1,0:T(8,128)S(1)}, f32[8,16,2048]{2,1,0:T(8,128)}, u32[]{:S(2)}) copy-start(f32[8,16,2048]{2,1,0:T(8,128)} %u_ref.7) | copy-start | bytes 3145732
  0.7 3.1 %copy-start.1 = (f32[8,16,2048]{2,1,0:T(8,128)S(1)}, f32[8,16,2048]{2,1,0:T(8,128)}, u32[]{:S(2)}) copy-start(f32[8,16,2048]{2,1,0:T(8,128)} %v_ref.7) | copy-start | bytes 3145732
  3.6 27.3 %collective-permute-start.6 = (f32[2,2,16,2048]{3,2,1,0:T(8,128)}, f32[2,2,16,2048]{3,2,1,0:T(8,128)S(1)}, u32[]{:S(2)}, u32[]{:S(2)}) collective-permute-start(f32[2,2,16,2048]{3,2,1,0:T(8,128)} %get-tuple-element.22), channel_id=1, source_target_pairs={{0,64},{64,0},{128,192},{192,128},{1,65},{65,1},{129,193},{193,129... | collective-permute-start | bytes 1572872 | tf_op jit(solution)/shard_map/ppermute | solution.py:443
  3.7 1.6 %copy-start.2 = (bf16[2,2,8,16,2048]{4,3,2,1,0:T(8,128)(2,1)S(1)}, bf16[2,2,8,16,2048]{4,3,2,1,0:T(8,128)(2,1)}, u32[]{:S(2)}) copy-start(bf16[2,2,8,16,2048]{4,3,2,1,0:T(8,128)(2,1)} %w_ref.3) | copy-start | bytes 6291460
  5.3 1.2 copy-start.4
  6.6 6.8 %copy-start.8 = (f32[2,2,16,2048]{3,2,1,0:T(8,128)S(1)}, f32[2,2,16,2048]{3,2,1,0:T(8,128)}, u32[]{:S(2)}) copy-start(f32[2,2,16,2048]{3,2,1,0:T(8,128)} %get-tuple-element.23) | copy-start | bytes 1572868
  6.6 9.8 %copy-start.7 = (f32[2,2,16,2048]{3,2,1,0:T(8,128)S(1)}, f32[2,2,16,2048]{3,2,1,0:T(8,128)}, u32[]{:S(2)}) copy-start(f32[2,2,16,2048]{3,2,1,0:T(8,128)} %get-tuple-element.24) | copy-start | bytes 1572868
  6.6 10.2 %copy-start.11 = (s32[8]{0:T(128)S(1)}, s32[8]{0:T(128)}, u32[]{:S(2)}) copy-start(s32[8]{0:T(128)} %param.10) | copy-start | bytes 100
  6.6 17.2 %copy-start.3 = (bf16[2,2,8,16,2048]{4,3,2,1,0:T(8,128)(2,1)S(1)}, bf16[2,2,8,16,2048]{4,3,2,1,0:T(8,128)(2,1)}, u32[]{:S(2)}) copy-start(bf16[2,2,8,16,2048]{4,3,2,1,0:T(8,128)(2,1)} %w_ref.3) | copy-start | bytes 6291460
  6.6 17.2 %copy-start.5 = (f32[8,16,2048]{2,1,0:T(8,128)S(1)}, f32[8,16,2048]{2,1,0:T(8,128)}, u32[]{:S(2)}) copy-start(f32[8,16,2048]{2,1,0:T(8,128)} %t_ref.3) | copy-start | bytes 3145732
  7.4 10.7 %collective-permute-start.4 = (f32[32,2048]{1,0:T(8,128)S(1)}, f32[32,2048]{1,0:T(8,128)S(1)}, u32[]{:S(2)}, u32[]{:S(2)}) collective-permute-start(f32[32,2048]{1,0:T(8,128)S(1)} %get-tuple-element.14), channel_id=1, source_target_pairs={{0,1},{1,2},{2,3},{3,4},{4,5},{5,6},{6,7},{7,8},{8,9},{9,10},{10,1... | collective-permute-start | bytes 786440 | tf_op jit(solution)/shard_map/ppermute | solution.py:455
  11.3 12.4 %collective-permute-start.5 = (f32[32,2048]{1,0:T(8,128)S(1)}, f32[32,2048]{1,0:T(8,128)S(1)}, u32[]{:S(2)}, u32[]{:S(2)}) collective-permute-start(f32[32,2048]{1,0:T(8,128)S(1)} %get-tuple-element.15), channel_id=1, source_target_pairs={{1,0},{2,1},{3,2},{4,3},{5,4},{6,5},{7,6},{8,7},{9,8},{10,9},{11,1... | collective-permute-start | bytes 786440 | tf_op jit(solution)/shard_map/ppermute | solution.py:456
  13.4 18.1 %collective-permute-start.1 = (f32[2,2,16,2048]{3,2,1,0:T(8,128)S(1)}, f32[2,2,16,2048]{3,2,1,0:T(8,128)S(1)}, u32[]{:S(2)}, u32[]{:S(2)}) collective-permute-start(f32[2,2,16,2048]{3,2,1,0:T(8,128)S(1)} %copy-done.8), channel_id=1, source_target_pairs={{0,192},{64,128},{128,64},{192,0},{1,193},{65,129},{129,65},{193,1... | collective-permute-start | bytes 1572872 | tf_op jit(solution)/shard_map/ppermute | solution.py:443
  16.3 24.4 %collective-permute-start = (f32[2,2,16,2048]{3,2,1,0:T(8,128)S(1)}, f32[2,2,16,2048]{3,2,1,0:T(8,128)S(1)}, u32[]{:S(2)}, u32[]{:S(2)}) collective-permute-start(f32[2,2,16,2048]{3,2,1,0:T(8,128)S(1)} %copy-done.7), channel_id=1, source_target_pairs={{0,128},{64,192},{128,0},{192,64},{1,129},{65,193},{129,1},{193,65... | collective-permute-start | bytes 1572872 | tf_op jit(solution)/shard_map/ppermute | solution.py:443
  27.4 34.6 %collective-permute-start.11 = (f32[2,2,16,2048]{3,2,1,0:T(8,128)S(1)}, f32[2,2,16,2048]{3,2,1,0:T(8,128)S(1)}, u32[]{:S(2)}, u32[]{:S(2)}) collective-permute-start(f32[2,2,16,2048]{3,2,1,0:T(8,128)S(1)} %get-tuple-element.21), channel_id=1, source_target_pairs={{0,64},{64,0},{128,192},{192,128},{1,65},{65,1},{129,193},{193,129... | collective-permute-start | bytes 1572872 | tf_op jit(solution)/shard_map/ppermute | solution.py:443
  27.5 36.2 %collective-permute-start.9 = (f32[2,2,16,2048]{3,2,1,0:T(8,128)S(1)}, f32[2,2,16,2048]{3,2,1,0:T(8,128)S(1)}, u32[]{:S(2)}, u32[]{:S(2)}) collective-permute-start(f32[2,2,16,2048]{3,2,1,0:T(8,128)S(1)} %get-tuple-element.18), channel_id=1, source_target_pairs={{0,128},{64,192},{128,0},{192,64},{1,129},{65,193},{129,1},{193,65... | collective-permute-start | bytes 1572872 | tf_op jit(solution)/shard_map/ppermute | solution.py:443
  30.8 32.9 %collective-permute-start.10 = (f32[2,2,16,2048]{3,2,1,0:T(8,128)S(1)}, f32[2,2,16,2048]{3,2,1,0:T(8,128)S(1)}, u32[]{:S(2)}, u32[]{:S(2)}) collective-permute-start(f32[2,2,16,2048]{3,2,1,0:T(8,128)S(1)} %get-tuple-element.19), channel_id=1, source_target_pairs={{0,192},{64,128},{128,64},{192,0},{1,193},{65,129},{129,65},{193,1... | collective-permute-start | bytes 1572872 | tf_op jit(solution)/shard_map/ppermute | solution.py:443
  31.6 12.5 %collective-permute-start.7 = (f32[16,2048]{1,0:T(8,128)S(1)}, f32[16,2048]{1,0:T(8,128)S(1)}, u32[]{:S(2)}, u32[]{:S(2)}) collective-permute-start(f32[16,2048]{1,0:T(8,128)S(1)} %get-tuple-element.16), channel_id=1, source_target_pairs={{0,1},{1,2},{2,3},{3,4},{4,5},{5,6},{6,7},{7,8},{8,9},{9,10},{10,1... | collective-permute-start | bytes 393224 | tf_op jit(solution)/shard_map/ppermute | solution.py:455
  40.7 9.1 %collective-permute-start.8 = (f32[16,2048]{1,0:T(8,128)S(1)}, f32[16,2048]{1,0:T(8,128)S(1)}, u32[]{:S(2)}, u32[]{:S(2)}) collective-permute-start(f32[16,2048]{1,0:T(8,128)S(1)} %get-tuple-element.17), channel_id=1, source_target_pairs={{1,0},{2,1},{3,2},{4,3},{5,4},{6,5},{7,6},{8,7},{9,8},{10,9},{11,1... | collective-permute-start | bytes 393224 | tf_op jit(solution)/shard_map/ppermute | solution.py:456
  44.1 10.9 %collective-permute-start.2 = (f32[16,2048]{1,0:T(8,128)S(1)}, f32[16,2048]{1,0:T(8,128)S(1)}, u32[]{:S(2)}, u32[]{:S(2)}) collective-permute-start(f32[16,2048]{1,0:T(8,128)S(1)} %get-tuple-element.12), channel_id=1, source_target_pairs={{0,1},{1,2},{2,3},{3,4},{4,5},{5,6},{6,7},{7,8},{8,9},{9,10},{10,1... | collective-permute-start | bytes 393224 | tf_op jit(solution)/shard_map/ppermute | solution.py:455
  49.8 9.0 %collective-permute-start.3 = (f32[16,2048]{1,0:T(8,128)S(1)}, f32[16,2048]{1,0:T(8,128)S(1)}, u32[]{:S(2)}, u32[]{:S(2)}) collective-permute-start(f32[16,2048]{1,0:T(8,128)S(1)} %get-tuple-element.13), channel_id=1, source_target_pairs={{1,0},{2,1},{3,2},{4,3},{5,4},{6,5},{7,6},{8,7},{9,8},{10,9},{11,1... | collective-permute-start | bytes 393224 | tf_op jit(solution)/shard_map/ppermute | solution.py:456
  65.4 74.2 %copy-start.6 = (f32[8]{0:T(128)S(1)}, f32[8]{0:T(128)}, u32[]{:S(2)}) copy-start(f32[8]{0:T(128)} %s.1) | copy-start | bytes 100

commit v3 on v2

--- a/solution.py
+++ b/solution.py
@@ -61,35 +61,37 @@
     return pl.BlockSpec(shape, lambda *args: (0,) * len(shape))
 
 
-def pack_static(scal, vx, vy, target, forcing):
+def pack_static(ids, scal, vx, vy, target, forcing):
     levels, rows, nx = target.shape
 
-    def body(s, u_ref, v_ref, t_ref, w_ref, up_ref, down_ref):
+    def body(q, s, u_ref, v_ref, t_ref, w_ref, up_ref, down_ref):
         for ref, r in ((up_ref, rows - 1), (down_ref, 0)):
+            for l in range(2):
+                ref[l : l + 1] = u_ref[l, r : r + 1]
+                ref[2 + l : 3 + l] = v_ref[l, r : r + 1]
             for l in range(levels):
-                ref[l : l + 1] = u_ref[l, r : r + 1]
-                ref[levels + l : levels + l + 1] = v_ref[l, r : r + 1]
                 nt = s[8 + l] * t_ref[l, r : r + 1]
                 for m in range(2):
                     w = w_ref[0, m, l, r : r + 1].astype(F32)
-                    i = (2 + m) * levels + l
+                    i = 4 + m * levels + l
                     ref[i : i + 1] = nt + forcing_scale * w
 
-    shape = (4 * levels, nx)
+    shape = (4 + 2 * levels, nx)
+    pair = pl.BlockSpec((2, rows, nx), lambda i, q, s: (q[8], 0, 0))
     out = jax.ShapeDtypeStruct(shape, F32)
     return pl.pallas_call(
         body,
         name="pack_static",
         out_shape=(out, out),
         grid_spec=pltpu.PrefetchScalarGridSpec(
-            num_scalar_prefetch=1,
+            num_scalar_prefetch=2,
             grid=(1,),
-            in_specs=[table(vx.shape)] * 3 + [table((1,) + forcing.shape[1:])],
+            in_specs=[pair, pair, table(target.shape), table((1,) + forcing.shape[1:])],
             out_specs=[table(shape)] * 2,
         ),
         compiler_params=params(16),
         cost_estimate=cost(0, 16 * target.size),
-    )(scal, vx, vy, target, forcing)
+    )(ids, scal, vx, vy, target, forcing)
 
 
 def pack_edges(ids, parts, limit):
@@ -129,7 +131,7 @@
 
 
 def twice(ids, scal, parts, vx, vy, halo, static, before):
-    level_count, rows, nx = vx.shape
+    _, rows, nx = vx.shape
     lanes = nx // 128
     base = 0 if before is None else 2
 
@@ -150,8 +152,8 @@
             cur_ref[...] = f1_ref[:, 0]
 
         def edge_row(ref, f, n, so):
-            u = ref[pl.ds(level, 1), :]
-            v = ref[pl.ds(level_count + level, 1), :]
+            u = ref[pl.ds(l, 1), :]
+            v = ref[pl.ds(2 + l, 1), :]
             east = pltpu.roll(f, nx - 1, 1)
             west = pltpu.roll(f, 1, 1)
             return combine(f, east, west, n, so, coefs_of(d, nu, u, v))
@@ -164,8 +166,8 @@
             n2 = above_ref[pl.ds(here + 1, 1), :]
             new_low = edge_row(sb_ref, s1, cur_ref[m, 0:1, :], s2)
             new_high = edge_row(sa_ref, n1, n2, cur_ref[m, rows - 1 : rows, :])
-            low_ref[0, m] = s1
-            high_ref[0, m] = n1
+            low_ref[0, m] = jnp.where(low_ok, s1, 0.0)
+            high_ref[0, m] = jnp.where(high_ok, n1, 0.0)
             low_ref[1, m] = jnp.where(low_ok, new_low, 0.0)
             high_ref[1, m] = jnp.where(high_ok, new_high, 0.0)
 
@@ -236,8 +238,9 @@
         level = 2 * (q[8] ^ k) + l
         d, nu = s[level], s[8 + level]
         for m in range(2):
-            low_ref[m] = below_ref[pl.ds((2 + m) * level_count + level, 1), :]
-            high_ref[m] = above_ref[pl.ds((2 + m) * level_count + level, 1), :]
+            row = pl.ds(4 + m * level_count + level, 1)
+            low_ref[m] = jnp.where(s[16] > 0.0, below_ref[row, :], 0.0)
+            high_ref[m] = jnp.where(s[17] > 0.0, above_ref[row, :], 0.0)
         for j in range(lanes):
             nt = nu * t_ref[0, :, at(j)]
             for m in range(2):
@@ -436,8 +439,8 @@
     rows, _ = ensemble.shape[2:]
     group = lax.axis_index("particle")
     tile = lax.axis_index("tile")
-    up = [(i, i + 1) for i in range(tiles - 1)]
-    down = [(i + 1, i) for i in range(tiles - 1)]
+    up = [(i, (i + 1) % tiles) for i in range(tiles)]
+    down = [(j, i) for i, j in up]
 
     def trade(value, k):
         return lax.ppermute(value, "particle", [(i, i ^ k) for i in range(4)])
@@ -456,7 +459,7 @@
         above = lax.ppermute(pair[1], "tile", down)
         return below, above
 
-    edges = pack_static(scal, velocity_x, northward_speed_ratio, target, forcing)
+    edges = pack_static(ids, scal, velocity_x, northward_speed_ratio, target, forcing)
     static = exchange(edges)
     edges = pack_edges(ids, parts[:2], 16)
     near = exchange(edges)

time: 145 us -> 134 us (0.924)
  starting transfers between devices: 25.9 us -> 12.8 us
  Pallas kernels: 18.8 us -> 23.2 us
  waiting for transfers between devices: 17 us -> 14.6 us
    ppermute x3, starting transfers between devices: 12.3 us -> 4.67 us  [exchange(): below = lax.ppermute(pair[0], 'tile', up)]
    ppermute x3, starting transfers between devices: 6.74 us -> 1.09 us  [exchange(): above = lax.ppermute(pair[1], 'tile', down)]
    ppermute x3, waiting for transfers between devices: 1.28 us -> 6.63 us  [exchange(): below = lax.ppermute(pair[0], 'tile', up)]
    ppermute x6, waiting for transfers between devices: 5.89 us -> 1.72 us  [trade(): return lax.ppermute(value, 'particle', [(i, i ^ k) for i in range(4)])]
    ppermute x3, waiting for transfers between devices: 9.8 us -> 6.3 us  [exchange(): above = lax.ppermute(pair[1], 'tile', down)]
    pallas_call x2, Pallas kernels: 6.6 us -> 8.87 us  [twice(): pl.pallas_call(body, name='twice', out_shape=jax.ShapeDtypeStruct((8, 2,...]
    pallas_call x2, Pallas kernels: 1.3 us -> 3.38 us  [pack_edges(): pl.pallas_call(body, name='pack_edges', out_shape=(out, out), grid_spec=p...]
  transfers between devices with their start and end apart: 12 -> 12, of which waited for: 5 -> 6; matrix products, arithmetic and copies ran while one was open for 0% -> 0% of each run, Pallas kernels for 10% -> 14%
where the time goes in v3:
time: 134 us; the launch traced here: 131 us
  blocking collectives  74 us (55%)
  Pallas kernels  23.2 us (17%)
  waiting for transfers between devices  14.6 us (11%)
  starting transfers between devices  12.8 us (10%)
  local copies, waits for them, and re-layouts  5.71 us (4%)
    all_to_all x1, blocking collectives, on_device(): lax.all_to_all(blocks.reshape(4 * tiles, rows, 128), ('particle', 'tile')...  74 us
    pallas_call x2, Pallas kernels, twice(): pl.pallas_call(body, name='twice', out_shape=jax.ShapeDtypeStruct((8, 2,...  8.87 us
    ppermute x6, starting transfers between devices, trade(): return lax.ppermute(value, 'particle', [(i, i ^ k) for i in range(4)])  7.09 us
    ppermute x3, waiting for transfers between devices, exchange(): below = lax.ppermute(pair[0], 'tile', up)  6.63 us
    ppermute x3, waiting for transfers between devices, exchange(): above = lax.ppermute(pair[1], 'tile', down)  6.3 us
    ppermute x3, starting transfers between devices, exchange(): below = lax.ppermute(pair[0], 'tile', up)  4.67 us
    pallas_call x1, Pallas kernels, driven(): pl.pallas_call(body, name='driven', out_shape=[jax.ShapeDtypeStruct((2, 2...  3.72 us
    pallas_call x2, Pallas kernels, pack_edges(): pl.pallas_call(body, name='pack_edges', out_shape=(out, out), grid_spec=p...  3.38 us
  transfers between devices with their start and end apart: 12, of which 6 were waited for; matrix products, arithmetic and copies ran while one was open for 0% of the time, Pallas kernels for 14%

profile of v3, /device:TPU:6, one launch (start us, length us, event | category | flops | bytes accessed | tf_op | source)
XLA Modules:
  0.0 131.4 jit_solution(14112201651351393505)
XLA Ops:
  0.7 2.9 %constant_dynamic-slice_fusion = (f32[2,2,16,2048]{3,2,1,0:T(8,128)}, f32[2,2,16,2048]{3,2,1,0:T(8,128)}, f32[2,2,16,2048]{3,2,1,0:T(8,128)}, f32[2,2,16,2048]{3,2,1,0:T(8,128)S(1)}) fusion(f32[2,8,16,2048]{3,2,1,0:T(8,128)} %param.9, s32[]{:T(128)S(6)} %select_n.15, s32[]{:T(128)S(6)} %select_n.13, s32[]{:T(128)S(6)} %select_n.12, s32[]{:T(128)S(6)} %select_n.14), kind=kLoop, calls=%fused_computation.1 | loop fusion | bytes 4194320 | tf_op jit(solution)/shard_map/dynamic_slice | solution.py:448
  3.6 3.3 %collective-permute-start.1 = (f32[2,2,16,2048]{3,2,1,0:T(8,128)}, f32[2,2,16,2048]{3,2,1,0:T(8,128)S(1)}, u32[]{:S(2)}, u32[]{:S(2)}) collective-permute-start(f32[2,2,16,2048]{3,2,1,0:T(8,128)} %get-tuple-element.23), channel_id=1, source_target_pairs={{0,192},{64,128},{128,64},{192,0},{1,193},{65,129},{129,65},{193,1... | collective-permute-start | bytes 1572872 | tf_op jit(solution)/shard_map/ppermute | solution.py:446
  6.9 0.3 collective-permute-start
  7.2 0.1 add_convert_fusion
  7.3 0.1 pad_add_fusion.s.q
  7.4 0.1 pad_maximum_fusion.s
  7.5 1.6 %copy-done.2 = bf16[2,2,8,16,2048]{4,3,2,1,0:T(8,128)(2,1)S(1)} copy-done((bf16[2,2,8,16,2048]{4,3,2,1,0:T(8,128)(2,1)S(1)}, bf16[2,2,8,16,2048]{4,3,2,1,0:T(8,128)(2,1)}, u32[]{:S(2)}) %copy-start.2) | copy-done | bytes 2097176
  9.1 1.2 copy-done.3
  10.3 0.8 pack_static.1
  11.1 1.9 %collective-permute-start.4 = (f32[20,2048]{1,0:T(8,128)S(1)}, f32[20,2048]{1,0:T(8,128)S(1)}, u32[]{:S(2)}, u32[]{:S(2)}) collective-permute-start(f32[20,2048]{1,0:T(8,128)S(1)} %get-tuple-element.14), channel_id=1, source_target_pairs={{0,1},{1,2},{2,3},{3,4},{4,5},{5,6},{6,7},{7,8},{8,9},{9,10},{10,1... | collective-permute-start | bytes 491528 | tf_op jit(solution)/shard_map/ppermute | solution.py:458
  13.0 0.2 collective-permute-start.5
  13.2 4.6 %collective-permute-done.4.sb_ref.below_ref = f32[20,2048]{1,0:T(8,128)S(1)} collective-permute-done((f32[20,2048]{1,0:T(8,128)S(1)}, f32[20,2048]{1,0:T(8,128)S(1)}, u32[]{:S(2)}, u32[]{:S(2)}) %collective-permute-start.4) | collective-permute-done | bytes 163872 | tf_op jit(solution)/shard_map/ppermute | solution.py:458
  17.8 3.7 %collective-permute-done.5.sa_ref.above_ref = f32[20,2048]{1,0:T(8,128)S(1)} collective-permute-done((f32[20,2048]{1,0:T(8,128)S(1)}, f32[20,2048]{1,0:T(8,128)S(1)}, u32[]{:S(2)}, u32[]{:S(2)}) %collective-permute-start.5) | collective-permute-done | bytes 163872 | tf_op jit(solution)/shard_map/ppermute | solution.py:459
  21.4 3.7 %driven.1 = (f32[2,2,16,2048]{3,2,1,0:T(8,128)S(1)}, f32[2,2,16,2048]{3,2,1,0:T(8,128)S(1)}, f32[2,2,16,2048]{3,2,1,0:T(8,128)S(1)}, f32[2,2,16,2048]{3,2,1,0:T(8,128)S(1)}) custom-call(s32[9]{0:T(128)S(1)} %pad_add_fusion.s.q, f32[18]{0:T(128)S(1)} %pad_maximum_fusion.s, f32[8,16,2048]{2,1,0:T(8,128)S(1)} %copy-done, f32[8,16,2048]{2,1,0:T(8,128)S(1)} %copy-done.1, ...), custom_call_target="tpu_custom_call" | custom-call | flops 20971520 | bytes 7340032 | tf_op jit(solution)/shard_map/driven/pallas_call | solution.py:278
  25.2 0.1 collective-permute-start.11
  25.3 3.2 %collective-permute-start.9 = (f32[2,2,16,2048]{3,2,1,0:T(8,128)S(1)}, f32[2,2,16,2048]{3,2,1,0:T(8,128)S(1)}, u32[]{:S(2)}, u32[]{:S(2)}) collective-permute-start(f32[2,2,16,2048]{3,2,1,0:T(8,128)S(1)} %get-tuple-element.18), channel_id=1, source_target_pairs={{0,128},{64,192},{128,0},{192,64},{1,129},{65,193},{129,1},{193,65... | collective-permute-start | bytes 1572872 | tf_op jit(solution)/shard_map/ppermute | solution.py:446
  28.5 0.1 collective-permute-start.10
  28.6 1.7 %pack_edges.3 = (f32[16,2048]{1,0:T(8,128)S(1)}, f32[16,2048]{1,0:T(8,128)S(1)}) custom-call(s32[9]{0:T(128)S(1)} %pad_add_fusion.s.q, f32[2,2,16,2048]{3,2,1,0:T(8,128)S(1)} %get-tuple-element.25.refs_0_.f0_ref, f32[2,2,16,2048]{3,2,1,0:T(8,128)} %collective-permute-done.6.refs_1_.f1_ref), custom_call_target="tpu_custom_call" | custom-call | bytes 1048576 | tf_op jit(solution)/shard_map/pack_edges/pallas_call | solution.py:118
  30.3 0.4 collective-permute-start.7
  30.7 0.9 collective-permute-done.refs_0_.f0_ref
  31.5 0.9 collective-permute-start.8
  32.4 1.7 %pack_edges.2 = (f32[16,2048]{1,0:T(8,128)S(1)}, f32[16,2048]{1,0:T(8,128)S(1)}) custom-call(s32[9]{0:T(128)S(1)} %pad_add_fusion.s.q, f32[2,2,16,2048]{3,2,1,0:T(8,128)} %collective-permute-done.refs_0_.f0_ref, f32[2,2,16,2048]{3,2,1,0:T(8,128)S(1)} %collective-permute-done.1.refs_1_.f1_ref), custom_call_target="tpu_custom_call" | custom-call | bytes 1048576 | tf_op jit(solution)/shard_map/pack_edges/pallas_call | solution.py:118
  34.1 2.1 %collective-permute-done.7.below_ref = f32[16,2048]{1,0:T(8,128)S(1)} collective-permute-done((f32[16,2048]{1,0:T(8,128)S(1)}, f32[16,2048]{1,0:T(8,128)S(1)}, u32[]{:S(2)}, u32[]{:S(2)}) %collective-permute-start.7) | collective-permute-done | bytes 131104 | tf_op jit(solution)/shard_map/ppermute | solution.py:458
  36.2 2.4 %collective-permute-start.2 = (f32[16,2048]{1,0:T(8,128)S(1)}, f32[16,2048]{1,0:T(8,128)S(1)}, u32[]{:S(2)}, u32[]{:S(2)}) collective-permute-start(f32[16,2048]{1,0:T(8,128)S(1)} %get-tuple-element.12), channel_id=1, source_target_pairs={{0,1},{1,2},{2,3},{3,4},{4,5},{5,6},{6,7},{7,8},{8,9},{9,10},{10,1... | collective-permute-start | bytes 393224 | tf_op jit(solution)/shard_map/ppermute | solution.py:458
  38.6 4.5 %twice.2.rest_0_ = f32[8,2,16,2048]{3,2,1,0:T(8,128)S(1)} custom-call(s32[9]{0:T(128)S(1)} %pad_add_fusion.s.q, f32[18]{0:T(128)S(1)} %pad_maximum_fusion.s, f32[2,2,16,2048]{3,2,1,0:T(8,128)S(1)} %get-tuple-element.25.refs_0_.f0_ref, f32[2,2,16,2048]{3,2,1,0:T(8,128)} %collective-permute-done.6.refs_1_.f1_ref, f32[8,16,2048]{2,1,0:T(8,128)S(1)} %copy-done, ...), custom_call_target="tpu_custom_call" | custom-call | flops 15728640 | bytes 3145728 | tf_op jit(solution)/shard_map/twice/pallas_call | solution.py:209
  43.1 2.6 %collective-permute-done.3.above_ref = f32[16,2048]{1,0:T(8,128)S(1)} collective-permute-done((f32[16,2048]{1,0:T(8,128)S(1)}, f32[16,2048]{1,0:T(8,128)S(1)}, u32[]{:S(2)}, u32[]{:S(2)}) %collective-permute-start.3) | collective-permute-done | bytes 131104 | tf_op jit(solution)/shard_map/ppermute | solution.py:459
  45.7 4.4 %twice.3.f0_ref.f1_ref = f32[8,2,16,2048]{3,2,1,0:T(8,128)S(1)} custom-call(s32[9]{0:T(128)S(1)} %pad_add_fusion.s.q, f32[18]{0:T(128)S(1)} %pad_maximum_fusion.s, f32[2,2,16,2048]{3,2,1,0:T(8,128)} %collective-permute-done.refs_0_.f0_ref, f32[2,2,16,2048]{3,2,1,0:T(8,128)S(1)} %collective-permute-done.1.refs_1_.f1_ref, ...), custom_call_target="tpu_custom_call", output_to_operand_aliasing={{}: (10, {})} | custom-call | flops 15728640 | bytes 3145728 | tf_op jit(solution)/shard_map/twice/pallas_call | solution.py:209
  50.1 1.7 %assemble.2.rest_0_ = f32[4,64,16,128]{3,2,1,0:T(8,128)S(1)} custom-call(s32[9]{0:T(128)S(1)} %pad_add_fusion.s.q, f32[8,2,16,2048]{3,2,1,0:T(8,128)S(1)} %twice.3.f0_ref.f1_ref, f32[8,2,16,2048]{3,2,1,0:T(8,128)S(1)} %twice.3.f0_ref.f1_ref, f32[2,2,16,2048]{3,2,1,0:T(8,128)S(1)} %get-tuple-element.20.r0_ref, ...), custom_call_target="tpu_custom_call" | custom-call | flops 524288 | bytes 4194304 | tf_op jit(solution)/shard_map/assemble/pallas_call | solution.py:350
  51.8 0.8 collective-permute-done.10.r1_ref
  52.7 1.6 %assemble.3 = f32[4,64,16,128]{3,2,1,0:T(8,128)S(1)} custom-call(s32[9]{0:T(128)S(1)} %pad_add_fusion.s.q, f32[8,2,16,2048]{3,2,1,0:T(8,128)S(1)} %twice.3.f0_ref.f1_ref, f32[8,2,16,2048]{3,2,1,0:T(8,128)S(1)} %twice.3.f0_ref.f1_ref, f32[2,2,16,2048]{3,2,1,0:T(8,128)S(1)} %collective-permute-done.9.r0_ref, ...), custom_call_target="tpu_custom_call", output_to_operand_aliasing={{}: (5, {})} | custom-call | flops 524288 | bytes 4194304 | tf_op jit(solution)/shard_map/assemble/pallas_call | solution.py:350
  54.3 74.0 %all_to_all.5 = f32[256,16,128]{2,1,0:T(8,128)S(1)} all-to-all(f32[256,16,128]{2,1,0:T(8,128)S(1)} %bitcast.5), channel_id=1, replica_groups=mesh['particle'=4,'tile'=64] {'particle','tile'}, dimensions={0} | all-to-all | bytes 4194304 | tf_op jit(solution)/shard_map/all_to_all | solution.py:482
  128.3 3.1 %finish.1 = (f32[2,8,32,1024]{3,2,1,0:T(8,128)}, f32[2,32,1024]{2,1,0:T(8,128)}) custom-call(f32[8]{0:T(128)S(1)} %copy-done.4, f32[4,64,16,128]{3,2,1,0:T(8,128)S(1)} %bitcast.6), custom_call_target="tpu_custom_call" | custom-call | flops 10485760 | bytes 6291456 | tf_op jit(solution)/shard_map/finish/pallas_call | solution.py:405
  (22 shorter events, 0.1 us)
Async XLA Ops:
  0.7 6.6 %copy-start.7 = (s32[8]{0:T(128)S(1)}, s32[8]{0:T(128)}, u32[]{:S(2)}) copy-start(s32[8]{0:T(128)} %param.10) | copy-start | bytes 100
  0.7 6.7 %copy-start.5 = (f32[8]{0:T(128)S(1)}, f32[8]{0:T(128)}, u32[]{:S(2)}) copy-start(f32[8]{0:T(128)} %param.16) | copy-start | bytes 100
  0.7 6.7 %copy-start.6 = (f32[8]{0:T(128)S(1)}, f32[8]{0:T(128)}, u32[]{:S(2)}) copy-start(f32[8]{0:T(128)} %param.15) | copy-start | bytes 100
  0.7 6.8 %copy-start = (f32[8,16,2048]{2,1,0:T(8,128)S(1)}, f32[8,16,2048]{2,1,0:T(8,128)}, u32[]{:S(2)}) copy-start(f32[8,16,2048]{2,1,0:T(8,128)} %u_ref.7) | copy-start | bytes 3145732
  0.7 6.8 %copy-start.1 = (f32[8,16,2048]{2,1,0:T(8,128)S(1)}, f32[8,16,2048]{2,1,0:T(8,128)}, u32[]{:S(2)}) copy-start(f32[8,16,2048]{2,1,0:T(8,128)} %v_ref.7) | copy-start | bytes 3145732
  3.6 24.9 %collective-permute-start.6 = (f32[2,2,16,2048]{3,2,1,0:T(8,128)}, f32[2,2,16,2048]{3,2,1,0:T(8,128)}, u32[]{:S(2)}, u32[]{:S(2)}) collective-permute-start(f32[2,2,16,2048]{3,2,1,0:T(8,128)} %get-tuple-element.22), channel_id=1, source_target_pairs={{0,64},{64,0},{128,192},{192,128},{1,65},{65,1},{129,193},{193,129... | collective-permute-start | bytes 1572872 | tf_op jit(solution)/shard_map/ppermute | solution.py:446
  3.6 26.7 %collective-permute-start.1 = (f32[2,2,16,2048]{3,2,1,0:T(8,128)}, f32[2,2,16,2048]{3,2,1,0:T(8,128)S(1)}, u32[]{:S(2)}, u32[]{:S(2)}) collective-permute-start(f32[2,2,16,2048]{3,2,1,0:T(8,128)} %get-tuple-element.23), channel_id=1, source_target_pairs={{0,192},{64,128},{128,64},{192,0},{1,193},{65,129},{129,65},{193,1... | collective-permute-start | bytes 1572872 | tf_op jit(solution)/shard_map/ppermute | solution.py:446
  6.9 24.7 %collective-permute-start = (f32[2,2,16,2048]{3,2,1,0:T(8,128)}, f32[2,2,16,2048]{3,2,1,0:T(8,128)}, u32[]{:S(2)}, u32[]{:S(2)}) collective-permute-start(f32[2,2,16,2048]{3,2,1,0:T(8,128)} %get-tuple-element.24), channel_id=1, source_target_pairs={{0,128},{64,192},{128,0},{192,64},{1,129},{65,193},{129,1},{193,65... | collective-permute-start | bytes 1572872 | tf_op jit(solution)/shard_map/ppermute | solution.py:446
  7.5 1.6 %copy-start.2 = (bf16[2,2,8,16,2048]{4,3,2,1,0:T(8,128)(2,1)S(1)}, bf16[2,2,8,16,2048]{4,3,2,1,0:T(8,128)(2,1)}, u32[]{:S(2)}) copy-start(bf16[2,2,8,16,2048]{4,3,2,1,0:T(8,128)(2,1)} %w_ref.3) | copy-start | bytes 6291460
  9.1 1.2 copy-start.3
  11.1 6.7 %collective-permute-start.4 = (f32[20,2048]{1,0:T(8,128)S(1)}, f32[20,2048]{1,0:T(8,128)S(1)}, u32[]{:S(2)}, u32[]{:S(2)}) collective-permute-start(f32[20,2048]{1,0:T(8,128)S(1)} %get-tuple-element.14), channel_id=1, source_target_pairs={{0,1},{1,2},{2,3},{3,4},{4,5},{5,6},{6,7},{7,8},{8,9},{9,10},{10,1... | collective-permute-start | bytes 491528 | tf_op jit(solution)/shard_map/ppermute | solution.py:458
  13.0 8.4 %collective-permute-start.5 = (f32[20,2048]{1,0:T(8,128)S(1)}, f32[20,2048]{1,0:T(8,128)S(1)}, u32[]{:S(2)}, u32[]{:S(2)}) collective-permute-start(f32[20,2048]{1,0:T(8,128)S(1)} %get-tuple-element.15), channel_id=1, source_target_pairs={{1,0},{2,1},{3,2},{4,3},{5,4},{6,5},{7,6},{8,7},{9,8},{10,9},{11,1... | collective-permute-start | bytes 491528 | tf_op jit(solution)/shard_map/ppermute | solution.py:459
  25.2 25.0 %collective-permute-start.11 = (f32[2,2,16,2048]{3,2,1,0:T(8,128)S(1)}, f32[2,2,16,2048]{3,2,1,0:T(8,128)S(1)}, u32[]{:S(2)}, u32[]{:S(2)}) collective-permute-start(f32[2,2,16,2048]{3,2,1,0:T(8,128)S(1)} %get-tuple-element.21), channel_id=1, source_target_pairs={{0,64},{64,0},{128,192},{192,128},{1,65},{65,1},{129,193},{193,129... | collective-permute-start | bytes 1572872 | tf_op jit(solution)/shard_map/ppermute | solution.py:446
  25.3 26.5 %collective-permute-start.9 = (f32[2,2,16,2048]{3,2,1,0:T(8,128)S(1)}, f32[2,2,16,2048]{3,2,1,0:T(8,128)S(1)}, u32[]{:S(2)}, u32[]{:S(2)}) collective-permute-start(f32[2,2,16,2048]{3,2,1,0:T(8,128)S(1)} %get-tuple-element.18), channel_id=1, source_target_pairs={{0,128},{64,192},{128,0},{192,64},{1,129},{65,193},{129,1},{193,65... | collective-permute-start | bytes 1572872 | tf_op jit(solution)/shard_map/ppermute | solution.py:446
  28.5 24.2 %collective-permute-start.10 = (f32[2,2,16,2048]{3,2,1,0:T(8,128)S(1)}, f32[2,2,16,2048]{3,2,1,0:T(8,128)S(1)}, u32[]{:S(2)}, u32[]{:S(2)}) collective-permute-start(f32[2,2,16,2048]{3,2,1,0:T(8,128)S(1)} %get-tuple-element.19), channel_id=1, source_target_pairs={{0,192},{64,128},{128,64},{192,0},{1,193},{65,129},{129,65},{193,1... | collective-permute-start | bytes 1572872 | tf_op jit(solution)/shard_map/ppermute | solution.py:446
  30.3 5.9 %collective-permute-start.7 = (f32[16,2048]{1,0:T(8,128)S(1)}, f32[16,2048]{1,0:T(8,128)S(1)}, u32[]{:S(2)}, u32[]{:S(2)}) collective-permute-start(f32[16,2048]{1,0:T(8,128)S(1)} %get-tuple-element.16), channel_id=1, source_target_pairs={{0,1},{1,2},{2,3},{3,4},{4,5},{5,6},{6,7},{7,8},{8,9},{9,10},{10,1... | collective-permute-start | bytes 393224 | tf_op jit(solution)/shard_map/ppermute | solution.py:458
  31.5 7.1 %collective-permute-start.8 = (f32[16,2048]{1,0:T(8,128)S(1)}, f32[16,2048]{1,0:T(8,128)S(1)}, u32[]{:S(2)}, u32[]{:S(2)}) collective-permute-start(f32[16,2048]{1,0:T(8,128)S(1)} %get-tuple-element.17), channel_id=1, source_target_pairs={{1,0},{2,1},{3,2},{4,3},{5,4},{6,5},{7,6},{8,7},{9,8},{10,9},{11,1... | collective-permute-start | bytes 393224 | tf_op jit(solution)/shard_map/ppermute | solution.py:459
  36.2 6.9 %collective-permute-start.2 = (f32[16,2048]{1,0:T(8,128)S(1)}, f32[16,2048]{1,0:T(8,128)S(1)}, u32[]{:S(2)}, u32[]{:S(2)}) collective-permute-start(f32[16,2048]{1,0:T(8,128)S(1)} %get-tuple-element.12), channel_id=1, source_target_pairs={{0,1},{1,2},{2,3},{3,4},{4,5},{5,6},{6,7},{7,8},{8,9},{9,10},{10,1... | collective-permute-start | bytes 393224 | tf_op jit(solution)/shard_map/ppermute | solution.py:458
  38.6 7.1 %collective-permute-start.3 = (f32[16,2048]{1,0:T(8,128)S(1)}, f32[16,2048]{1,0:T(8,128)S(1)}, u32[]{:S(2)}, u32[]{:S(2)}) collective-permute-start(f32[16,2048]{1,0:T(8,128)S(1)} %get-tuple-element.13), channel_id=1, source_target_pairs={{1,0},{2,1},{3,2},{4,3},{5,4},{6,5},{7,6},{8,7},{9,8},{10,9},{11,1... | collective-permute-start | bytes 393224 | tf_op jit(solution)/shard_map/ppermute | solution.py:459
  54.3 74.0 %copy-start.4 = (f32[8]{0:T(128)S(1)}, f32[8]{0:T(128)}, u32[]{:S(2)}) copy-start(f32[8]{0:T(128)} %s.1) | copy-start | bytes 100

commit v4 on v3

--- a/solution.py
+++ b/solution.py
@@ -445,8 +445,14 @@
     def trade(value, k):
         return lax.ppermute(value, "particle", [(i, i ^ k) for i in range(4)])
 
-    pieces = [lax.dynamic_slice_in_dim(ensemble, 2 * (group ^ k), 2, axis=1) for k in range(4)]
-    parts = [pieces[0], None, None, None]
+    def cut(value, k):
+        return lax.dynamic_slice_in_dim(value, 2 * (group ^ k), 2, axis=1)
+
+    parts = [None] * 4
+    pieces = (cut(ensemble, 2), cut(ensemble, 3))
+    held, *pieces = lax.optimization_barrier((ensemble, *pieces))
+    pieces = [cut(held, 0), cut(held, 1), *pieces]
+    parts[0] = pieces[0]
     for k in (3, 2, 1):
         parts[k] = trade(pieces[k], k)
 

time: 134 us -> 136 us (1.015)
  local copies, waits for them, and re-layouts: 5.71 us -> 7.37 us
    dynamic_slice x1 -> x2, local copies, waits for them, and re-layouts: 2.87 us -> 4.53 us  [cut(): return lax.dynamic_slice_in_dim(value, 2 * (group ^ k), 2, axis=1)]
  transfers between devices with their start and end apart: 12 -> 12, of which waited for: 6 -> 5; matrix products, arithmetic and copies ran while one was open for 0% -> 0% of each run, Pallas kernels for 14% -> 14%
where the time goes in v4:
time: 136 us; the launch traced here: 133 us
  blocking collectives  74 us (54%)
  Pallas kernels  23.2 us (17%)
  waiting for transfers between devices  14.2 us (10%)
  starting transfers between devices  13.4 us (10%)
  local copies, waits for them, and re-layouts  7.37 us (5%)
    all_to_all x1, blocking collectives, on_device(): lax.all_to_all(blocks.reshape(4 * tiles, rows, 128), ('particle', 'tile')...  74 us
    pallas_call x2, Pallas kernels, twice(): pl.pallas_call(body, name='twice', out_shape=jax.ShapeDtypeStruct((8, 2,...  8.92 us
    ppermute x3, waiting for transfers between devices, exchange(): below = lax.ppermute(pair[0], 'tile', up)  7.13 us
    ppermute x6, starting transfers between devices, trade(): return lax.ppermute(value, 'particle', [(i, i ^ k) for i in range(4)])  6.81 us
    ppermute x3, waiting for transfers between devices, exchange(): above = lax.ppermute(pair[1], 'tile', down)  6.26 us
    ppermute x3, starting transfers between devices, exchange(): below = lax.ppermute(pair[0], 'tile', up)  4.67 us
    dynamic_slice x2, local copies, waits for them, and re-layouts, cut(): return lax.dynamic_slice_in_dim(value, 2 * (group ^ k), 2, axis=1)  4.53 us
    pallas_call x1, Pallas kernels, driven(): pl.pallas_call(body, name='driven', out_shape=[jax.ShapeDtypeStruct((2, 2...  3.72 us
  transfers between devices with their start and end apart: 12, of which 5 were waited for; matrix products, arithmetic and copies ran while one was open for 0% of the time, Pallas kernels for 14%

profile of v4, /device:TPU:6, one launch (start us, length us, event | category | flops | bytes accessed | tf_op | source)
XLA Modules:
  0.0 133.2 jit_solution(4596787655276795636)
XLA Ops:
  0.7 2.4 %constant_dynamic-slice_fusion.2 = (f32[2,2,16,2048]{3,2,1,0:T(8,128)}, f32[2,2,16,2048]{3,2,1,0:T(8,128)}) fusion(f32[2,8,16,2048]{3,2,1,0:T(8,128)} %param.9, s32[]{:T(128)S(6)} %select_n.13, s32[]{:T(128)S(6)} %select_n.12), kind=kLoop, calls=%fused_computation.3 | loop fusion | bytes 2097160 | tf_op jit(solution)/shard_map/dynamic_slice | solution.py:449
  3.1 2.1 %constant_dynamic-slice_fusion = (f32[2,2,16,2048]{3,2,1,0:T(8,128)}, f32[2,2,16,2048]{3,2,1,0:T(8,128)S(1)}) fusion(f32[2,8,16,2048]{3,2,1,0:T(8,128)} %param.9, s32[]{:T(128)S(6)} %select_n.15, s32[]{:T(128)S(6)} %select_n.14), kind=kLoop, calls=%fused_computation.1 | loop fusion | bytes 2097160 | tf_op jit(solution)/shard_map/dynamic_slice | solution.py:449
  5.2 3.2 %collective-permute-start = (f32[2,2,16,2048]{3,2,1,0:T(8,128)}, f32[2,2,16,2048]{3,2,1,0:T(8,128)S(1)}, u32[]{:S(2)}, u32[]{:S(2)}) collective-permute-start(f32[2,2,16,2048]{3,2,1,0:T(8,128)} %get-tuple-element.15), channel_id=1, source_target_pairs={{0,128},{64,192},{128,0},{192,64},{1,129},{65,193},{129,1},{193,65... | collective-permute-start | bytes 1572872 | tf_op jit(solution)/shard_map/ppermute | solution.py:446
  8.4 0.2 collective-permute-start.1
  8.6 0.1 add_convert_fusion
  8.7 0.1 pad_add_fusion.s.q
  8.8 0.1 pad_maximum_fusion.s
  8.8 1.6 %copy-done.2 = bf16[2,2,8,16,2048]{4,3,2,1,0:T(8,128)(2,1)S(1)} copy-done((bf16[2,2,8,16,2048]{4,3,2,1,0:T(8,128)(2,1)S(1)}, bf16[2,2,8,16,2048]{4,3,2,1,0:T(8,128)(2,1)}, u32[]{:S(2)}) %copy-start.2) | copy-done | bytes 2097176
  10.4 1.2 copy-done.3
  11.7 0.8 pack_static.1
  12.5 1.9 %collective-permute-start.4 = (f32[20,2048]{1,0:T(8,128)S(1)}, f32[20,2048]{1,0:T(8,128)S(1)}, u32[]{:S(2)}, u32[]{:S(2)}) collective-permute-start(f32[20,2048]{1,0:T(8,128)S(1)} %get-tuple-element.19), channel_id=1, source_target_pairs={{0,1},{1,2},{2,3},{3,4},{4,5},{5,6},{6,7},{7,8},{8,9},{9,10},{10,1... | collective-permute-start | bytes 491528 | tf_op jit(solution)/shard_map/ppermute | solution.py:464
  14.4 0.2 collective-permute-start.5
  14.6 5.1 %collective-permute-done.4.sb_ref.below_ref = f32[20,2048]{1,0:T(8,128)S(1)} collective-permute-done((f32[20,2048]{1,0:T(8,128)S(1)}, f32[20,2048]{1,0:T(8,128)S(1)}, u32[]{:S(2)}, u32[]{:S(2)}) %collective-permute-start.4) | collective-permute-done | bytes 163872 | tf_op jit(solution)/shard_map/ppermute | solution.py:464
  19.6 3.7 %collective-permute-done.5.sa_ref.above_ref = f32[20,2048]{1,0:T(8,128)S(1)} collective-permute-done((f32[20,2048]{1,0:T(8,128)S(1)}, f32[20,2048]{1,0:T(8,128)S(1)}, u32[]{:S(2)}, u32[]{:S(2)}) %collective-permute-start.5) | collective-permute-done | bytes 163872 | tf_op jit(solution)/shard_map/ppermute | solution.py:465
  23.3 3.7 %driven.1 = (f32[2,2,16,2048]{3,2,1,0:T(8,128)S(1)}, f32[2,2,16,2048]{3,2,1,0:T(8,128)S(1)}, f32[2,2,16,2048]{3,2,1,0:T(8,128)S(1)}, f32[2,2,16,2048]{3,2,1,0:T(8,128)S(1)}) custom-call(s32[9]{0:T(128)S(1)} %pad_add_fusion.s.q, f32[18]{0:T(128)S(1)} %pad_maximum_fusion.s, f32[8,16,2048]{2,1,0:T(8,128)S(1)} %copy-done, f32[8,16,2048]{2,1,0:T(8,128)S(1)} %copy-done.1, ...), custom_call_target="tpu_custom_call" | custom-call | flops 20971520 | bytes 7340032 | tf_op jit(solution)/shard_map/driven/pallas_call | solution.py:278
  27.0 0.1 collective-permute-start.11
  27.1 3.3 %collective-permute-start.9 = (f32[2,2,16,2048]{3,2,1,0:T(8,128)S(1)}, f32[2,2,16,2048]{3,2,1,0:T(8,128)S(1)}, u32[]{:S(2)}, u32[]{:S(2)}) collective-permute-start(f32[2,2,16,2048]{3,2,1,0:T(8,128)S(1)} %get-tuple-element.24), channel_id=1, source_target_pairs={{0,128},{64,192},{128,0},{192,64},{1,129},{65,193},{129,1},{193,65... | collective-permute-start | bytes 1572872 | tf_op jit(solution)/shard_map/ppermute | solution.py:446
  30.4 0.1 collective-permute-start.10
  30.5 1.7 %pack_edges.3 = (f32[16,2048]{1,0:T(8,128)S(1)}, f32[16,2048]{1,0:T(8,128)S(1)}) custom-call(s32[9]{0:T(128)S(1)} %pad_add_fusion.s.q, f32[2,2,16,2048]{3,2,1,0:T(8,128)S(1)} %get-tuple-element.29.refs_0_.f0_ref, f32[2,2,16,2048]{3,2,1,0:T(8,128)} %collective-permute-done.6.refs_1_.f1_ref), custom_call_target="tpu_custom_call" | custom-call | bytes 1048576 | tf_op jit(solution)/shard_map/pack_edges/pallas_call | solution.py:118
  32.2 0.4 collective-permute-start.7
  32.6 1.7 %collective-permute-start.8 = (f32[16,2048]{1,0:T(8,128)S(1)}, f32[16,2048]{1,0:T(8,128)S(1)}, u32[]{:S(2)}, u32[]{:S(2)}) collective-permute-start(f32[16,2048]{1,0:T(8,128)S(1)} %get-tuple-element.23), channel_id=1, source_target_pairs={{1,0},{2,1},{3,2},{4,3},{5,4},{6,5},{7,6},{8,7},{9,8},{10,9},{11,1... | collective-permute-start | bytes 393224 | tf_op jit(solution)/shard_map/ppermute | solution.py:465
  34.3 1.7 %pack_edges.2 = (f32[16,2048]{1,0:T(8,128)S(1)}, f32[16,2048]{1,0:T(8,128)S(1)}) custom-call(s32[9]{0:T(128)S(1)} %pad_add_fusion.s.q, f32[2,2,16,2048]{3,2,1,0:T(8,128)S(1)} %collective-permute-done.refs_0_.f0_ref, f32[2,2,16,2048]{3,2,1,0:T(8,128)} %collective-permute-done.1.refs_1_.f1_ref), custom_call_target="tpu_custom_call" | custom-call | bytes 1048576 | tf_op jit(solution)/shard_map/pack_edges/pallas_call | solution.py:118
  36.0 2.1 %collective-permute-done.7.below_ref = f32[16,2048]{1,0:T(8,128)S(1)} collective-permute-done((f32[16,2048]{1,0:T(8,128)S(1)}, f32[16,2048]{1,0:T(8,128)S(1)}, u32[]{:S(2)}, u32[]{:S(2)}) %collective-permute-start.7) | collective-permute-done | bytes 131104 | tf_op jit(solution)/shard_map/ppermute | solution.py:464
  38.1 2.4 %collective-permute-start.2 = (f32[16,2048]{1,0:T(8,128)S(1)}, f32[16,2048]{1,0:T(8,128)S(1)}, u32[]{:S(2)}, u32[]{:S(2)}) collective-permute-start(f32[16,2048]{1,0:T(8,128)S(1)} %get-tuple-element.17), channel_id=1, source_target_pairs={{0,1},{1,2},{2,3},{3,4},{4,5},{5,6},{6,7},{7,8},{8,9},{9,10},{10,1... | collective-permute-start | bytes 393224 | tf_op jit(solution)/shard_map/ppermute | solution.py:464
  40.5 4.5 %twice.2.rest_0_ = f32[8,2,16,2048]{3,2,1,0:T(8,128)S(1)} custom-call(s32[9]{0:T(128)S(1)} %pad_add_fusion.s.q, f32[18]{0:T(128)S(1)} %pad_maximum_fusion.s, f32[2,2,16,2048]{3,2,1,0:T(8,128)S(1)} %get-tuple-element.29.refs_0_.f0_ref, f32[2,2,16,2048]{3,2,1,0:T(8,128)} %collective-permute-done.6.refs_1_.f1_ref, f32[8,16,2048]{2,1,0:T(8,128)S(1)} %copy-done, ...), custom_call_target="tpu_custom_call" | custom-call | flops 15728640 | bytes 3145728 | tf_op jit(solution)/shard_map/twice/pallas_call | solution.py:209
  44.9 2.6 %collective-permute-done.3.above_ref = f32[16,2048]{1,0:T(8,128)S(1)} collective-permute-done((f32[16,2048]{1,0:T(8,128)S(1)}, f32[16,2048]{1,0:T(8,128)S(1)}, u32[]{:S(2)}, u32[]{:S(2)}) %collective-permute-start.3) | collective-permute-done | bytes 131104 | tf_op jit(solution)/shard_map/ppermute | solution.py:465
  47.5 4.5 %twice.3.f0_ref.f1_ref = f32[8,2,16,2048]{3,2,1,0:T(8,128)S(1)} custom-call(s32[9]{0:T(128)S(1)} %pad_add_fusion.s.q, f32[18]{0:T(128)S(1)} %pad_maximum_fusion.s, f32[2,2,16,2048]{3,2,1,0:T(8,128)S(1)} %collective-permute-done.refs_0_.f0_ref, f32[2,2,16,2048]{3,2,1,0:T(8,128)} %collective-permute-done.1.refs_1_.f1_ref, ...), custom_call_target="tpu_custom_call", output_to_operand_aliasing={{}: (10, {})} | custom-call | flops 15728640 | bytes 3145728 | tf_op jit(solution)/shard_map/twice/pallas_call | solution.py:209
  52.0 1.7 %assemble.2.rest_0_ = f32[4,64,16,128]{3,2,1,0:T(8,128)S(1)} custom-call(s32[9]{0:T(128)S(1)} %pad_add_fusion.s.q, f32[8,2,16,2048]{3,2,1,0:T(8,128)S(1)} %twice.3.f0_ref.f1_ref, f32[8,2,16,2048]{3,2,1,0:T(8,128)S(1)} %twice.3.f0_ref.f1_ref, f32[2,2,16,2048]{3,2,1,0:T(8,128)S(1)} %get-tuple-element.26.r0_ref, ...), custom_call_target="tpu_custom_call" | custom-call | flops 524288 | bytes 4194304 | tf_op jit(solution)/shard_map/assemble/pallas_call | solution.py:350
  53.7 0.8 collective-permute-done.10.r1_ref
  54.5 1.6 %assemble.3 = f32[4,64,16,128]{3,2,1,0:T(8,128)S(1)} custom-call(s32[9]{0:T(128)S(1)} %pad_add_fusion.s.q, f32[8,2,16,2048]{3,2,1,0:T(8,128)S(1)} %twice.3.f0_ref.f1_ref, f32[8,2,16,2048]{3,2,1,0:T(8,128)S(1)} %twice.3.f0_ref.f1_ref, f32[2,2,16,2048]{3,2,1,0:T(8,128)S(1)} %collective-permute-done.9.r0_ref, ...), custom_call_target="tpu_custom_call", output_to_operand_aliasing={{}: (5, {})} | custom-call | flops 524288 | bytes 4194304 | tf_op jit(solution)/shard_map/assemble/pallas_call | solution.py:350
  56.2 74.0 %all_to_all.5 = f32[256,16,128]{2,1,0:T(8,128)S(1)} all-to-all(f32[256,16,128]{2,1,0:T(8,128)S(1)} %bitcast.5), channel_id=1, replica_groups=mesh['particle'=4,'tile'=64] {'particle','tile'}, dimensions={0} | all-to-all | bytes 4194304 | tf_op jit(solution)/shard_map/all_to_all | solution.py:488
  130.1 3.1 %finish.1 = (f32[2,8,32,1024]{3,2,1,0:T(8,128)}, f32[2,32,1024]{2,1,0:T(8,128)}) custom-call(f32[8]{0:T(128)S(1)} %copy-done.4, f32[4,64,16,128]{3,2,1,0:T(8,128)S(1)} %bitcast.6), custom_call_target="tpu_custom_call" | custom-call | flops 10485760 | bytes 6291456 | tf_op jit(solution)/shard_map/finish/pallas_call | solution.py:405
  (23 shorter events, 0.1 us)
Async XLA Ops:
  0.7 8.0 %copy-start.7 = (s32[8]{0:T(128)S(1)}, s32[8]{0:T(128)}, u32[]{:S(2)}) copy-start(s32[8]{0:T(128)} %param.10) | copy-start | bytes 100
  0.7 8.1 %copy-start.5 = (f32[8]{0:T(128)S(1)}, f32[8]{0:T(128)}, u32[]{:S(2)}) copy-start(f32[8]{0:T(128)} %param.16) | copy-start | bytes 100
  0.7 8.1 %copy-start.6 = (f32[8]{0:T(128)S(1)}, f32[8]{0:T(128)}, u32[]{:S(2)}) copy-start(f32[8]{0:T(128)} %param.15) | copy-start | bytes 100
  0.7 8.2 %copy-start = (f32[8,16,2048]{2,1,0:T(8,128)S(1)}, f32[8,16,2048]{2,1,0:T(8,128)}, u32[]{:S(2)}) copy-start(f32[8,16,2048]{2,1,0:T(8,128)} %u_ref.7) | copy-start | bytes 3145732
  0.7 8.1 %copy-start.1 = (f32[8,16,2048]{2,1,0:T(8,128)S(1)}, f32[8,16,2048]{2,1,0:T(8,128)}, u32[]{:S(2)}) copy-start(f32[8,16,2048]{2,1,0:T(8,128)} %v_ref.7) | copy-start | bytes 3145732
  5.2 25.2 %collective-permute-start.6 = (f32[2,2,16,2048]{3,2,1,0:T(8,128)}, f32[2,2,16,2048]{3,2,1,0:T(8,128)}, u32[]{:S(2)}, u32[]{:S(2)}) collective-permute-start(f32[2,2,16,2048]{3,2,1,0:T(8,128)} %get-tuple-element.28), channel_id=1, source_target_pairs={{0,64},{64,0},{128,192},{192,128},{1,65},{65,1},{129,193},{193,129... | collective-permute-start | bytes 1572872 | tf_op jit(solution)/shard_map/ppermute | solution.py:446
  5.2 27.0 %collective-permute-start = (f32[2,2,16,2048]{3,2,1,0:T(8,128)}, f32[2,2,16,2048]{3,2,1,0:T(8,128)S(1)}, u32[]{:S(2)}, u32[]{:S(2)}) collective-permute-start(f32[2,2,16,2048]{3,2,1,0:T(8,128)} %get-tuple-element.15), channel_id=1, source_target_pairs={{0,128},{64,192},{128,0},{192,64},{1,129},{65,193},{129,1},{193,65... | collective-permute-start | bytes 1572872 | tf_op jit(solution)/shard_map/ppermute | solution.py:446
  8.4 24.1 %collective-permute-start.1 = (f32[2,2,16,2048]{3,2,1,0:T(8,128)}, f32[2,2,16,2048]{3,2,1,0:T(8,128)}, u32[]{:S(2)}, u32[]{:S(2)}) collective-permute-start(f32[2,2,16,2048]{3,2,1,0:T(8,128)} %get-tuple-element.16), channel_id=1, source_target_pairs={{0,192},{64,128},{128,64},{192,0},{1,193},{65,129},{129,65},{193,1... | collective-permute-start | bytes 1572872 | tf_op jit(solution)/shard_map/ppermute | solution.py:446
  8.8 1.6 %copy-start.2 = (bf16[2,2,8,16,2048]{4,3,2,1,0:T(8,128)(2,1)S(1)}, bf16[2,2,8,16,2048]{4,3,2,1,0:T(8,128)(2,1)}, u32[]{:S(2)}) copy-start(bf16[2,2,8,16,2048]{4,3,2,1,0:T(8,128)(2,1)} %w_ref.3) | copy-start | bytes 6291460
  10.4 1.2 copy-start.3
  12.5 7.2 %collective-permute-start.4 = (f32[20,2048]{1,0:T(8,128)S(1)}, f32[20,2048]{1,0:T(8,128)S(1)}, u32[]{:S(2)}, u32[]{:S(2)}) collective-permute-start(f32[20,2048]{1,0:T(8,128)S(1)} %get-tuple-element.19), channel_id=1, source_target_pairs={{0,1},{1,2},{2,3},{3,4},{4,5},{5,6},{6,7},{7,8},{8,9},{9,10},{10,1... | collective-permute-start | bytes 491528 | tf_op jit(solution)/shard_map/ppermute | solution.py:464
  14.4 8.9 %collective-permute-start.5 = (f32[20,2048]{1,0:T(8,128)S(1)}, f32[20,2048]{1,0:T(8,128)S(1)}, u32[]{:S(2)}, u32[]{:S(2)}) collective-permute-start(f32[20,2048]{1,0:T(8,128)S(1)} %get-tuple-element.20), channel_id=1, source_target_pairs={{1,0},{2,1},{3,2},{4,3},{5,4},{6,5},{7,6},{8,7},{9,8},{10,9},{11,1... | collective-permute-start | bytes 491528 | tf_op jit(solution)/shard_map/ppermute | solution.py:465
  27.0 25.0 %collective-permute-start.11 = (f32[2,2,16,2048]{3,2,1,0:T(8,128)S(1)}, f32[2,2,16,2048]{3,2,1,0:T(8,128)S(1)}, u32[]{:S(2)}, u32[]{:S(2)}) collective-permute-start(f32[2,2,16,2048]{3,2,1,0:T(8,128)S(1)} %get-tuple-element.27), channel_id=1, source_target_pairs={{0,64},{64,0},{128,192},{192,128},{1,65},{65,1},{129,193},{193,129... | collective-permute-start | bytes 1572872 | tf_op jit(solution)/shard_map/ppermute | solution.py:446
  27.1 26.5 %collective-permute-start.9 = (f32[2,2,16,2048]{3,2,1,0:T(8,128)S(1)}, f32[2,2,16,2048]{3,2,1,0:T(8,128)S(1)}, u32[]{:S(2)}, u32[]{:S(2)}) collective-permute-start(f32[2,2,16,2048]{3,2,1,0:T(8,128)S(1)} %get-tuple-element.24), channel_id=1, source_target_pairs={{0,128},{64,192},{128,0},{192,64},{1,129},{65,193},{129,1},{193,65... | collective-permute-start | bytes 1572872 | tf_op jit(solution)/shard_map/ppermute | solution.py:446
  30.4 24.1 %collective-permute-start.10 = (f32[2,2,16,2048]{3,2,1,0:T(8,128)S(1)}, f32[2,2,16,2048]{3,2,1,0:T(8,128)S(1)}, u32[]{:S(2)}, u32[]{:S(2)}) collective-permute-start(f32[2,2,16,2048]{3,2,1,0:T(8,128)S(1)} %get-tuple-element.25), channel_id=1, source_target_pairs={{0,192},{64,128},{128,64},{192,0},{1,193},{65,129},{129,65},{193,1... | collective-permute-start | bytes 1572872 | tf_op jit(solution)/shard_map/ppermute | solution.py:446
  32.2 5.9 %collective-permute-start.7 = (f32[16,2048]{1,0:T(8,128)S(1)}, f32[16,2048]{1,0:T(8,128)S(1)}, u32[]{:S(2)}, u32[]{:S(2)}) collective-permute-start(f32[16,2048]{1,0:T(8,128)S(1)} %get-tuple-element.22), channel_id=1, source_target_pairs={{0,1},{1,2},{2,3},{3,4},{4,5},{5,6},{6,7},{7,8},{8,9},{9,10},{10,1... | collective-permute-start | bytes 393224 | tf_op jit(solution)/shard_map/ppermute | solution.py:464
  32.6 7.9 %collective-permute-start.8 = (f32[16,2048]{1,0:T(8,128)S(1)}, f32[16,2048]{1,0:T(8,128)S(1)}, u32[]{:S(2)}, u32[]{:S(2)}) collective-permute-start(f32[16,2048]{1,0:T(8,128)S(1)} %get-tuple-element.23), channel_id=1, source_target_pairs={{1,0},{2,1},{3,2},{4,3},{5,4},{6,5},{7,6},{8,7},{9,8},{10,9},{11,1... | collective-permute-start | bytes 393224 | tf_op jit(solution)/shard_map/ppermute | solution.py:465
  38.1 6.9 %collective-permute-start.2 = (f32[16,2048]{1,0:T(8,128)S(1)}, f32[16,2048]{1,0:T(8,128)S(1)}, u32[]{:S(2)}, u32[]{:S(2)}) collective-permute-start(f32[16,2048]{1,0:T(8,128)S(1)} %get-tuple-element.17), channel_id=1, source_target_pairs={{0,1},{1,2},{2,3},{3,4},{4,5},{5,6},{6,7},{7,8},{8,9},{9,10},{10,1... | collective-permute-start | bytes 393224 | tf_op jit(solution)/shard_map/ppermute | solution.py:464
  40.5 7.1 %collective-permute-start.3 = (f32[16,2048]{1,0:T(8,128)S(1)}, f32[16,2048]{1,0:T(8,128)S(1)}, u32[]{:S(2)}, u32[]{:S(2)}) collective-permute-start(f32[16,2048]{1,0:T(8,128)S(1)} %get-tuple-element.18), channel_id=1, source_target_pairs={{1,0},{2,1},{3,2},{4,3},{5,4},{6,5},{7,6},{8,7},{9,8},{10,9},{11,1... | collective-permute-start | bytes 393224 | tf_op jit(solution)/shard_map/ppermute | solution.py:465
  56.2 74.0 %copy-start.4 = (f32[8]{0:T(128)S(1)}, f32[8]{0:T(128)}, u32[]{:S(2)}) copy-start(f32[8]{0:T(128)} %s.1) | copy-start | bytes 100
